TPU v7x, 128 devices: a whole 4x4x4 slice. The times are simulated.
128 devices in a mesh: row: 8 (over y_lo, z), col: 16 (over y_hi, x, core).
Axes of the slice: x: 4, y: 4 (y_hi: 2, y_lo: 2; y = y_hi * 2 + y_lo), z: 4, core: 2. Of those that a mesh axis runs over, the one named last changes fastest.
Arguments:
- species: float32 [53, 64, 128, 256], P(None, 'row', 'col'), may hold values from 0.05 to 2
- velocity: float32 [3, 64, 128, 256], P(None, 'row', 'col'), may hold values from -1 to 1
- diffusivity: float32 [53], replicated, may hold values from 0.02 to 0.1
- divergence: float32 [64, 128, 256], P('row', 'col'), may hold values from -6 to 6
- log_rates: float32 [325], replicated, may hold values from -3 to 1
- reactants: int32 [325, 53], replicated, may hold values from 0 to 3, as said below
- products: int32 [325, 53], replicated, may hold values from 0 to 3, as said below
- heat_weights: float32 [53], replicated, may hold values from -0.875 to 0.875
- substeps: int32 [64, 128, 2], P('row', 'col'), may hold values from 1 to 6
Outputs:
- reacted: float32 [53, 64, 128, 256], P(None, 'row', 'col')
- pressure: float32 [64, 128, 256], P('row', 'col')
Inputs may be any that keep to these rules, and one draw needn't show every extreme that they name: `reactants`: each reaction has one or two reactant species. `products`: each reaction has one or two product species.
All inputs are finite; a program needn't handle non-finite values.
Results may differ from a plain program's by a relative error of at most 0.0003.
Values sent between devices are 32-bit elements; how exact they have to be, the bound alone decides.
A program may use at most 128 MiB of HBM per device.

v0:
```python
import functools
import math

import jax
import jax.numpy as jnp
from jax import lax
from jax.experimental import pallas as pl
from jax.experimental.pallas import tpu as pltpu
from jax.sharding import Mesh
from jax.sharding import PartitionSpec as P

BLOCK = 128
ROW = ("row_0", "row_1")
COL = ("col_0", "col_1", "col_2")
ROW_COL = ("row_0", "row_1", "col_0", "col_1", "col_2")
time_step = 0.2
screen = 0.004
highest = lax.Precision.HIGHEST

NS, NR = 53, 325
SP, RP = 56, 336
LOG2E = 1.4426950408889634
f32, bf16 = jnp.float32, jnp.bfloat16

def split3(x):
    hi = lax.reduce_precision(x, 8, 7)
    mid = lax.reduce_precision(x - hi, 8, 7)
    return hi, mid, x - hi - mid

def matrices(log_rates, reactants, products):
    rf = reactants.astype(f32)
    pf = products.astype(f32)
    bias = jnp.stack(split3(log_rates * LOG2E), axis=1)
    first = jnp.concatenate([rf, bias, rf, jnp.zeros((NR, 3), f32)], axis=1)
    first = jnp.pad(first, ((0, RP - NR), (0, 0))).astype(bf16)
    half = jnp.concatenate([jnp.pad(pf, ((0, RP - NR), (0, 3))), jnp.pad(rf, ((0, RP - NR), (0, 3)))], axis=1).T
    second = jnp.concatenate([half, half], axis=1).astype(bf16)
    return first, second

def kernel(G, first_flag_ref, counts_ref, sp_ref, xlo_ref, xhi_ref, ylo_ref, yhi_ref, vel_ref, diff_ref, heat_ref, div_ref, hrow_ref, nrow_ref,
           s1_ref, s2_ref, out_ref, src_ref, sp, hx, ext, mov, cur, outs, order_ref, hist_ref, sem):
    copies = []
    for z in range(2):
        c = pltpu.make_async_copy(sp_ref.at[:, pl.ds(z * 128, 128)], sp.at[z], sem.at[z])
        c.start(); copies.append(c)
    for k, r in enumerate((xlo_ref, xhi_ref, ylo_ref, yhi_ref)):
        for z in range(2):
            c = pltpu.make_async_copy(r.at[:, pl.ds(z * 128, 128)], hx.at[k, z], sem.at[2 + 2 * k + z])
            c.start(); copies.append(c)
    for k in range(8):
        hist_ref[k] = 0
    def count(i, _):
        n = counts_ref[i]
        hist_ref[n] = hist_ref[n] + 1
        return 0
    lax.fori_loop(0, 128, count, 0)
    base = jnp.int32(0)
    for n in range(6, 0, -1):
        here = hist_ref[n]
        hist_ref[n] = base
        base = base + here
    def place(i, _):
        n = counts_ref[i]
        at = hist_ref[n]
        order_ref[at] = i
        hist_ref[n] = at + 1
        return 0
    lax.fori_loop(0, 128, place, 0)
    for c in copies:
        c.wait()

    pad = jnp.full((SP - NS, 128), 2.0, f32)
    def lay(c, _):
        x = c // 8
        y = c % 8
        for z in range(2):
            ext[(x + 1) * 10 + y + 1, :NS, z * 128:(z + 1) * 128] = sp[z, pl.ds(c, NS, stride=64), :]
        return 0
    lax.fori_loop(0, 64, lay, 0)
    def edge(c, _):
        for k, at, own in ((0, c + 1, 10 + c + 1), (1, 90 + c + 1, 80 + c + 1), (2, (c + 1) * 10, (c + 1) * 10 + 1), (3, (c + 1) * 10 + 9, (c + 1) * 10 + 8)):
            flag = first_flag_ref[k]
            for z in range(2):
                zs = slice(z * 128, (z + 1) * 128)
                @pl.when(flag == 0)
                def _():
                    ext[at, :NS, zs] = hx[k, z, pl.ds(c, NS, stride=8), :]
                @pl.when(flag != 0)
                def _():
                    ext[at, :NS, zs] = ext[own, :NS, zs]
        return 0
    lax.fori_loop(0, 8, edge, 0)

    diff = jnp.broadcast_to(diff_ref[...], (SP, 256))
    lane = lax.broadcasted_iota(jnp.int32, (SP, 256), 1)
    row = lax.broadcasted_iota(jnp.int32, (SP, 256), 0)
    def move(c, _):
        x = c // 8
        y = c % 8
        e = (x + 1) * 10 + y + 1
        centre = ext[e]
        xm, xp, ym, yp = ext[e - 10], ext[e + 10], ext[e - 1], ext[e + 1]
        zm = jnp.where(lane == 0, centre, pltpu.roll(centre, 1, 1))
        zp = jnp.where(lane == 255, centre, pltpu.roll(centre, 255, 1))
        lateral = xm + xp + (ym + yp) + (zm + zp) - 6.0 * centre
        carried = None
        for d, (m, p) in enumerate(((xm, xp), (ym, yp), (zm, zp))):
            v = jnp.broadcast_to(vel_ref[d, pl.ds(c, 1), :], (SP, 256))
            t = jnp.maximum(v, 0.0) * (centre - m) + jnp.minimum(v, 0.0) * (p - centre)
            carried = t if carried is None else carried + t
        moved = centre + 0.2 * (diff * lateral - carried)
        moved = jnp.where(row < NS, moved, 2.0)
        mov[2 * c] = moved[:, :128]
        mov[2 * c + 1] = moved[:, 128:]
        return 0
    lax.fori_loop(0, 64, move, 0)

    W = G * 128
    heat = jnp.broadcast_to(heat_ref[...], (SP, 128))
    def turn(t, _):
        ids = [order_ref[t * G + j] for j in range(G)]
        top = counts_ref[ids[0]]
        for j in range(G):
            cur[:, j * 128:(j + 1) * 128] = mov[ids[j]]
        h = jnp.concatenate([hrow_ref[pl.ds(ids[j], 1), :] for j in range(G)], axis=1)
        n = jnp.concatenate([nrow_ref[pl.ds(ids[j], 1), :] for j in range(G)], axis=1)
        hb = jnp.broadcast_to(h, (SP, W))
        nb = jnp.broadcast_to(n, (SP, W))
        def level(k, _):
            conc = cur[...]
            lg = jnp.log2(conc)
            hi = lg.astype(bf16).astype(f32)
            xin = jnp.concatenate([hi, lg - hi], axis=0).astype(bf16)
            rates = jnp.exp2(jnp.dot(s1_ref[...], xin, preferred_element_type=f32))
            rhi = rates.astype(bf16)
            rlo = (rates - rhi.astype(f32)).astype(bf16)
            both = jnp.dot(s2_ref[...], jnp.concatenate([rhi, rlo], axis=0), preferred_element_type=f32)
            gained, lost = both[:SP], both[SP:]
            fresh = conc * (conc + hb * gained) / (conc + hb * lost)
            cur[...] = jnp.where(nb > k, fresh, conc)
            return 0
        lax.fori_loop(0, top, level, 0)
        for j in range(G):
            c = ids[j] // 2
            z = ids[j] % 2
            res = cur[:, j * 128:(j + 1) * 128]
            outs[z, pl.ds(c, NS, stride=64), :] = res[:NS]
            gain = jnp.sum(heat * (res - mov[ids[j]]), axis=0, keepdims=True)
            src_ref[pl.ds(ids[j], 1), :] = div_ref[pl.ds(ids[j], 1), :] - gain / 0.2
        return 0
    lax.fori_loop(0, 128 // G, turn, 0)
    copies = []
    for z in range(2):
        c = pltpu.make_async_copy(outs.at[z], out_ref.at[:, pl.ds(z * 128, 128)], sem.at[z])
        c.start(); copies.append(c)
    for c in copies:
        c.wait()

def call(G, flags, counts, species, faces, velocity, diffusivity, heat_weights, divergence, first, second):
    hrow = jnp.broadcast_to((0.2 / counts.astype(f32))[:, None], (128, 128))
    nrow = jnp.broadcast_to(counts[:, None], (128, 128))
    vm = pl.BlockSpec(memory_space=pltpu.VMEM)
    sm = pl.BlockSpec(memory_space=pltpu.SMEM)
    hb = pl.BlockSpec(memory_space=pl.ANY)
    out, src = pl.pallas_call(
        functools.partial(kernel, G),
        out_shape=(jax.ShapeDtypeStruct((NS * 64, 256), f32), jax.ShapeDtypeStruct((128, 128), f32)),
        in_specs=[sm, sm, hb, hb, hb, hb, hb] + [vm] * 8,
        out_specs=(hb, vm),
        scratch_shapes=[
            pltpu.VMEM((2, NS * 64, 128), f32), pltpu.VMEM((4, 2, NS * 8, 128), f32), pltpu.VMEM((100, SP, 256), f32), pltpu.VMEM((128, SP, 128), f32),
            pltpu.VMEM((SP, G * 128), f32), pltpu.VMEM((2, NS * 64, 128), f32), pltpu.SMEM((128,), jnp.int32), pltpu.SMEM((8,), jnp.int32), pltpu.SemaphoreType.DMA((10,))],
        compiler_params=pltpu.CompilerParams(vmem_limit_bytes=50 << 20),
        name="transport_kinetics",
    )(flags, counts, species.reshape(NS * 64, 256), *[f.reshape(NS * 8, 256) for f in faces], velocity.reshape(3, 64, 256),
      jnp.pad(diffusivity, (0, SP - NS))[:, None], jnp.pad(heat_weights, (0, SP - NS))[:, None], divergence.reshape(128, 128), hrow, nrow, first, second)
    return out.reshape(NS, 8, 8, 256), src.reshape(64, 256)


def split_up(x, dim, size):
    before, after = (x.shape[:dim], x.shape[dim + 1 :])
    return jnp.moveaxis(x.reshape(*before, size, -1, *after), dim, 0)


def joined_along(parts, dim):
    shape = list(parts.shape[1:])
    shape[dim] *= parts.shape[0]
    return jnp.moveaxis(parts, 0, dim).reshape(shape)


def turned_blocks(parts, axes, turns):
    inside = parts.shape[1:]
    result = parts.reshape(*(lax.axis_size(a) for a in axes), *inside)
    for k in turns:
        result = lax.all_to_all(result, axes[k], k, k, tiled=True)
    return result.reshape(-1, *inside)


def core_and_chips(x, groups, turns, split_dim, concat_dim):
    size = lax.axis_size(groups[0]) * lax.axis_size(groups[1])
    parts = split_up(x, split_dim, size)
    return joined_along(turned_blocks(parts, groups, turns), concat_dim)


def cosine_table(length):
    wave = jnp.arange(length, dtype=jnp.float32)
    sample = jnp.arange(length, dtype=jnp.float32) + 0.5
    weight = jnp.where(wave == 0, jnp.sqrt(1.0 / length), jnp.sqrt(2.0 / length)).astype(
        jnp.float32
    )
    return weight[:, None] * jnp.cos(jnp.pi * wave[:, None] * sample[None, :] / length)


def mode_values(length):
    wave = jnp.arange(length, dtype=jnp.float32)
    return 2.0 - 2.0 * jnp.cos(jnp.pi * wave / length)


def faces_of(x, axis, dim):
    size = lax.axis_size(axis)
    up = [(i, (i + 1) % size) for i in range(size - 1)]
    last = lax.index_in_dim(x, x.shape[dim] - 1, dim, keepdims=False)
    leading = lax.index_in_dim(x, 0, dim, keepdims=False)
    return lax.ppermute(last, axis, up), lax.ppermute(leading, axis, [(b, a) for a, b in up])


def local(species, velocity, diffusivity, divergence, log_rates, reactants, products, heat_weights, substeps):
    species_count, cells_x, cells_y, cells_z = species.shape
    rows_count = lax.axis_size(ROW)
    cols_count = lax.axis_size(COL)
    device_count = rows_count * cols_count
    x_low, x_high = faces_of(species, ROW, 1)
    y_low, y_high = faces_of(species, COL, 2)
    at_row, at_col = lax.axis_index(ROW), lax.axis_index(COL)
    flags = jnp.stack([at_row == 0, at_row == rows_count - 1, at_col == 0, at_col == cols_count - 1]).astype(jnp.int32)
    first, second = matrices(log_rates, reactants, products)
    reacted, source = call(8, flags, substeps.reshape(-1), species, (x_low, x_high, y_low, y_high), velocity, diffusivity, heat_weights, divergence, first, second)
    source = source.reshape(cells_x, cells_y, cells_z)
    table_z = cosine_table(cells_z)
    forward = jnp.einsum("kz,xyz->kxy", table_z, source, precision=highest).reshape(
        cells_z, cells_x * cells_y
    )
    planes = core_and_chips(forward, (("row_0", "row_1", "col_0", "col_1"), "col_2"), (0, 1), 0, 1)
    depth = cells_z // device_count
    planes = planes.reshape(depth, rows_count, cols_count, cells_x, cells_y)
    table_x = cosine_table(rows_count * cells_x).reshape(rows_count * cells_x, rows_count, cells_x)
    table_y = cosine_table(cols_count * cells_y).reshape(cols_count * cells_y, cols_count, cells_y)
    spectrum = jnp.einsum("ari,zrcij->zacj", table_x, planes, precision=highest)
    spectrum = jnp.einsum("bcj,zacj->zab", table_y, spectrum, precision=highest)
    device_index = lax.axis_index(ROW) * cols_count + lax.axis_index(COL)
    z_values = lax.dynamic_slice_in_dim(mode_values(cells_z), device_index * depth, depth, 0)
    denominator = (
        screen
        + z_values[:, None, None]
        + mode_values(rows_count * cells_x)[None, :, None]
        + mode_values(cols_count * cells_y)[None, None, :]
    )
    spectrum = spectrum / denominator
    spectrum = jnp.einsum("bcj,zab->zacj", table_y, spectrum, precision=highest)
    spectrum = jnp.einsum("ari,zacj->zrcij", table_x, spectrum, precision=highest)
    outgoing = spectrum.reshape(depth, device_count * cells_x * cells_y)
    columns = lax.all_to_all(outgoing, ROW_COL, split_axis=1, concat_axis=0, tiled=True)
    columns = columns.reshape(cells_z, cells_x, cells_y)
    pressure = jnp.einsum("kz,kxy->xyz", table_z, columns, precision=highest)
    return (reacted, pressure)


def solution(mesh):
    finer = Mesh(mesh.devices.reshape(2, 4, 2, 4, 2), ("row_0", "row_1", "col_0", "col_1", "col_2"))
    in_specs = (
        P(None, ROW, COL, None),
        P(None, ROW, COL, None),
        P(),
        P(ROW, COL, None),
        P(),
        P(),
        P(),
        P(),
        P(ROW, COL, None),
    )
    out_specs = (P(None, ROW, COL, None), P(ROW, COL, None))
    return jax.shard_map(local, mesh=finer, in_specs=in_specs, out_specs=out_specs, check_vma=False)
```

profile of v0, /device:TPU:1, one launch (start us, length us, event | category | flops | bytes accessed | tf_op | source)
XLA Modules:
  0.0 154.2 jit_solution(16109687992022002586)
XLA Ops:
  0.7 4.0 %fusion.44 = (f32[53,8,1,256]{3,2,1,0:T(1,128)S(1)}, f32[53,8,1,256]{3,2,1,0:T(1,128)S(1)}) fusion(f32[53,8,8,256]{3,2,1,0:T(8,128)} %param.9), kind=kLoop, calls=%fused_computation.83 | loop fusion | bytes 1736704 | tf_op jit(solution)/shard_map/slice | solution.py:223
  4.8 4.5 %collective-permute-start.2 = (f32[53,8,256]{2,1,0:T(8,128)S(1)}, f32[53,8,256]{2,1,0:T(8,128)S(1)}, u32[]{:S(2)}, u32[]{:S(2)}) collective-permute-start(f32[53,8,256]{2,1,0:T(8,128)S(1)} %bitcast.103), channel_id=1, source_target_pairs={{0,1},{1,2},{2,3},{3,4},{4,5},{5,6},{6,7},{7,8},{8,9},{9,10},{10,1... | collective-permute-start | bytes 1302536 | tf_op jit(solution)/shard_map/ppermute | solution.py:224
  9.3 1.9 %collective-permute-start.3 = (f32[53,8,256]{2,1,0:T(8,128)S(1)}, f32[53,8,256]{2,1,0:T(8,128)S(1)}, u32[]{:S(2)}, u32[]{:S(2)}) collective-permute-start(f32[53,8,256]{2,1,0:T(8,128)S(1)} %bitcast.104), channel_id=1, source_target_pairs={{1,0},{2,1},{3,2},{4,3},{5,4},{6,5},{7,6},{8,7},{9,8},{10,9},{11,1... | collective-permute-start | bytes 1302536 | tf_op jit(solution)/shard_map/ppermute | solution.py:224
  11.2 2.1 %slice_bitcast_fusion = (f32[53,8,256]{2,1,0:T(8,128)}, f32[53,8,256]{2,1,0:T(8,128)}) fusion(f32[53,8,8,256]{3,2,1,0:T(8,128)} %param.9), kind=kLoop, calls=%fused_computation.10 | loop fusion | bytes 1736704 | tf_op jit(solution)/shard_map/squeeze | solution.py:223
  13.3 3.6 %collective-permute-start = (f32[53,8,256]{2,1,0:T(8,128)}, f32[53,8,256]{2,1,0:T(8,128)S(1)}, u32[]{:S(2)}, u32[]{:S(2)}) collective-permute-start(f32[53,8,256]{2,1,0:T(8,128)} %get-tuple-element.9), channel_id=1, source_target_pairs={{0,16},{16,32},{32,48},{48,64},{64,80},{80,96},{96,112},{1,17},{17... | collective-permute-start | bytes 1302536 | tf_op jit(solution)/shard_map/ppermute | solution.py:224
  16.9 1.3 collective-permute-start.1
  18.6 0.1 concatenate.11
  18.7 0.1 copy.68
  18.8 0.1 copy.42
  18.9 0.1 reshape.199.counts_ref
  19.1 0.1 pad_maximum_fusion.s2_ref
  19.3 0.1 copy.45.diff_ref
  19.4 0.1 copy.46.heat_ref
  19.6 0.1 add_convert_fusion.first_flag_ref
  19.7 0.2 multiply_bitcast_fusion
  19.9 5.6 %collective-permute-done = f32[53,8,256]{2,1,0:T(8,128)S(1)} collective-permute-done((f32[53,8,256]{2,1,0:T(8,128)}, f32[53,8,256]{2,1,0:T(8,128)S(1)}, u32[]{:S(2)}, u32[]{:S(2)}) %collective-permute-start) | collective-permute-done | bytes 434208 | tf_op jit(solution)/shard_map/ppermute | solution.py:224
  25.6 4.0 %collective-permute-done.1 = f32[53,8,256]{2,1,0:T(8,128)S(1)} collective-permute-done((f32[53,8,256]{2,1,0:T(8,128)}, f32[53,8,256]{2,1,0:T(8,128)S(1)}, u32[]{:S(2)}, u32[]{:S(2)}) %collective-permute-start.1) | collective-permute-done | bytes 434208 | tf_op jit(solution)/shard_map/ppermute | solution.py:224
  29.7 0.1 broadcast_in_dim.63.nrow_ref
  29.8 38.3 %transport_kinetics.1 = (f32[3392,256]{1,0:T(8,128)}, f32[128,128]{1,0:T(8,128)S(1)}) custom-call(s32[4]{0:T(128)S(1)} %add_convert_fusion.first_flag_ref, s32[128]{0:T(128)S(1)} %reshape.199.counts_ref, f32[3392,256]{1,0:T(8,128)} %bitcast.98, f32[424,256]{1,0:T(8,128)S(1)} %bitcast.95, f32[424,256]{1,0:T(8,128)S(1)} %bitcast.96, f32[424,256]{1,0:T(8,128)S(1)} %bitcast.93, ...), custom_call_target="tpu_custom_call" | custom-call | tf_op jit(solution)/shard_map/transport_kinetics/pallas_call | solution.py:165
  68.1 1.3 fusion.9
  69.4 0.1 copy.48
  69.6 0.8 reshape.220
  70.3 43.6 %all-to-all-start = ((f32[64,1,256]{2,1,0:T(1,128)}), f32[64,1,256]{2,1,0:T(1,128)S(1)}, u32[]{:S(2)}, u32[]{:S(2)}) async-start(f32[64,1,256]{2,1,0:T(1,128)} %reshape.220), calls=%async_computation | async-start | bytes 131072 | tf_op jit(solution)/shard_map/all_to_all | solution.py:195
  113.9 8.4 %all-to-all-done = f32[64,1,256]{2,1,0:T(1,128)S(1)} async-done(((f32[64,1,256]{2,1,0:T(1,128)}), f32[64,1,256]{2,1,0:T(1,128)S(1)}, u32[]{:S(2)}, u32[]{:S(2)}) %all-to-all-start) | async-done | bytes 65568 | tf_op jit(solution)/shard_map/all_to_all | solution.py:195
  122.3 0.5 broadcast.225
  122.9 0.8 reduce
  123.7 0.1 reshape.221
  123.8 0.1 reshape.222
  124.0 6.1 %all_to_all.26 = f32[2,1,8192]{2,1,0:T(1,128)S(1)} all-to-all(f32[2,1,8192]{2,1,0:T(1,128)S(1)} %reshape.222), channel_id=1, replica_groups=mesh['row_0'=2,'row_1'=4,'col_0'=2,'col_1'=4,'col_2'=2] {'col_2'}, dimensions={0} | all-to-all | bytes 131072 | tf_op jit(solution)/shard_map/all_to_all | solution.py:195
  130.0 0.8 reduce.1
  130.9 0.2 reshape.223
  131.0 0.1 copy.50
  131.1 0.1 copy.51
  131.2 0.2 reshape_reshape.4
  131.4 1.0 convolution_bitcast_fusion.1
  132.4 0.5 fusion.1
  132.9 0.6 convolution_bitcast_fusion.2
  133.5 1.5 convolution_bitcast_fusion
  134.9 0.1 copy.54
  135.0 0.2 all_to_all.20
  135.2 0.1 copy.55
  135.3 0.8 reshape.224
  136.1 3.8 %all-to-all-start.2 = ((f32[128,1,128]{2,1,0:T(1,128)}), f32[128,1,128]{2,1,0:T(1,128)S(1)}, u32[]{:S(2)}, u32[]{:S(2)}) async-start(f32[128,1,128]{2,1,0:T(1,128)} %reshape.224), calls=%async_computation.2 | async-start | bytes 131072 | tf_op jit(solution)/shard_map/all_to_all | solution.py:262
  140.0 9.6 %all-to-all-done.2 = f32[128,1,128]{2,1,0:T(1,128)S(1)} async-done(((f32[128,1,128]{2,1,0:T(1,128)}), f32[128,1,128]{2,1,0:T(1,128)S(1)}, u32[]{:S(2)}, u32[]{:S(2)}) %all-to-all-start.2) | async-done | bytes 65568 | tf_op jit(solution)/shard_map/all_to_all | solution.py:262
  149.5 0.8 reduce.2
  150.3 0.1 reshape.225
  150.5 0.4 reshape.209
  150.9 3.3 %fusion.2 = f32[8,8,256]{2,1,0:T(8,128)} fusion(f32[256,8,8]{2,1,0:T(8,128)S(1)} %reshape.209, f32[256]{0:T(256)S(1)} %iota_add_fusion, f32[256]{0:T(256)S(1)} %get-tuple-element.22, f32[256]{0:T(256)S(1)} %get-tuple-element.21), kind=kOutput, calls=%fused_computation.6 | convolution fusion | flops 50528256 | bytes 134144 | tf_op jit(solution)/shard_map/kz,kxy->xyz/dot_general | solution.py:264
  (49 shorter events, 0.7 us)
Async XLA Ops:
  0.6 17.8 %copy-start.5 = (f32[325]{0:T(512)S(1)}, f32[325]{0:T(512)}, u32[]{:S(2)}) copy-start(f32[325]{0:T(512)} %param.13) | copy-start | bytes 3904
  0.6 17.9 %copy-start.1 = (s32[325,53]{0,1:T(8,128)S(1)}, s32[325,53]{0,1:T(8,128)}, u32[]{:S(2)}) copy-start(s32[325,53]{0,1:T(8,128)} %param.14) | copy-start | bytes 206704
  0.7 18.2 %copy-start.4 = (s32[8,8,2]{1,2,0:T(2,128)S(1)}, s32[8,8,2]{1,2,0:T(2,128)}, u32[]{:S(2)}) copy-start(s32[8,8,2]{1,2,0:T(2,128)} %param.17) | copy-start | bytes 1540
  0.7 18.4 %copy-start.2 = (s32[325,53]{0,1:T(8,128)S(1)}, s32[325,53]{0,1:T(8,128)}, u32[]{:S(2)}) copy-start(s32[325,53]{0,1:T(8,128)} %param.15) | copy-start | bytes 206704
  0.7 18.6 %copy-start.3 = (f32[8,8,256]{2,1,0:T(8,128)S(1)}, f32[8,8,256]{2,1,0:T(8,128)}, u32[]{:S(2)}) copy-start(f32[8,8,256]{2,1,0:T(8,128)} %param.12) | copy-start | bytes 196612
  0.7 18.6 %copy-start.6 = (f32[53]{0:T(128)S(1)}, f32[53]{0:T(128)}, u32[]{:S(2)}) copy-start(f32[53]{0:T(128)} %param.11) | copy-start | bytes 640
  0.7 18.7 %copy-start.7 = (f32[53]{0:T(128)S(1)}, f32[53]{0:T(128)}, u32[]{:S(2)}) copy-start(f32[53]{0:T(128)} %param.16) | copy-start | bytes 640
  0.7 29.1 %copy-start = (f32[3,8,8,256]{3,2,1,0:T(8,128)S(1)}, f32[3,8,8,256]{3,2,1,0:T(8,128)}, u32[]{:S(2)}) copy-start(f32[3,8,8,256]{3,2,1,0:T(8,128)} %param.10) | copy-start | bytes 589828
  4.8 15.2 %collective-permute-start.2 = (f32[53,8,256]{2,1,0:T(8,128)S(1)}, f32[53,8,256]{2,1,0:T(8,128)S(1)}, u32[]{:S(2)}, u32[]{:S(2)}) collective-permute-start(f32[53,8,256]{2,1,0:T(8,128)S(1)} %bitcast.103), channel_id=1, source_target_pairs={{0,1},{1,2},{2,3},{3,4},{4,5},{5,6},{6,7},{7,8},{8,9},{9,10},{10,1... | collective-permute-start | bytes 1302536 | tf_op jit(solution)/shard_map/ppermute | solution.py:224
  9.3 10.6 %collective-permute-start.3 = (f32[53,8,256]{2,1,0:T(8,128)S(1)}, f32[53,8,256]{2,1,0:T(8,128)S(1)}, u32[]{:S(2)}, u32[]{:S(2)}) collective-permute-start(f32[53,8,256]{2,1,0:T(8,128)S(1)} %bitcast.104), channel_id=1, source_target_pairs={{1,0},{2,1},{3,2},{4,3},{5,4},{6,5},{7,6},{8,7},{9,8},{10,9},{11,1... | collective-permute-start | bytes 1302536 | tf_op jit(solution)/shard_map/ppermute | solution.py:224
  13.3 12.2 %collective-permute-start = (f32[53,8,256]{2,1,0:T(8,128)}, f32[53,8,256]{2,1,0:T(8,128)S(1)}, u32[]{:S(2)}, u32[]{:S(2)}) collective-permute-start(f32[53,8,256]{2,1,0:T(8,128)} %get-tuple-element.9), channel_id=1, source_target_pairs={{0,16},{16,32},{32,48},{48,64},{64,80},{80,96},{96,112},{1,17},{17... | collective-permute-start | bytes 1302536 | tf_op jit(solution)/shard_map/ppermute | solution.py:224
  16.9 12.7 %collective-permute-start.1 = (f32[53,8,256]{2,1,0:T(8,128)}, f32[53,8,256]{2,1,0:T(8,128)S(1)}, u32[]{:S(2)}, u32[]{:S(2)}) collective-permute-start(f32[53,8,256]{2,1,0:T(8,128)} %get-tuple-element.8), channel_id=1, source_target_pairs={{16,0},{32,16},{48,32},{64,48},{80,64},{96,80},{112,96},{17,1},{33... | collective-permute-start | bytes 1302536 | tf_op jit(solution)/shard_map/ppermute | solution.py:224
  70.3 52.0 %all-to-all-start = ((f32[64,1,256]{2,1,0:T(1,128)}), f32[64,1,256]{2,1,0:T(1,128)S(1)}, u32[]{:S(2)}, u32[]{:S(2)}) async-start(f32[64,1,256]{2,1,0:T(1,128)} %reshape.220), calls=%async_computation | async-start | bytes 131072 | tf_op jit(solution)/shard_map/all_to_all | solution.py:195
  136.1 13.4 %all-to-all-start.2 = ((f32[128,1,128]{2,1,0:T(1,128)}), f32[128,1,128]{2,1,0:T(1,128)S(1)}, u32[]{:S(2)}, u32[]{:S(2)}) async-start(f32[128,1,128]{2,1,0:T(1,128)} %reshape.224), calls=%async_computation.2 | async-start | bytes 131072 | tf_op jit(solution)/shard_map/all_to_all | solution.py:262
where the time goes:
time: 155 us; the launch traced here: 154 us
  starting transfers between devices  58.7 us (38%)
  Pallas kernels  38.3 us (25%)
  waiting for transfers between devices  27.6 us (18%)
  local copies, waits for them, and re-layouts  11 us (7%)
  matrix products  8.11 us (5%)
  blocking collectives  6.05 us (4%)
  other arithmetic  3.19 us (2%)
    all_to_all x1, starting transfers between devices, turned_blocks(): result = lax.all_to_all(result, axes[k], k, k, tiled=True)  43.6 us
    pallas_call x1, Pallas kernels, call(): pl.pallas_call(functools.partial(kernel, G), out_shape=(jax.ShapeDtypeStr...  38.3 us
    all_to_all x1, waiting for transfers between devices, local(): lax.all_to_all(outgoing, ROW_COL, split_axis=1, concat_axis=0, tiled=True)  9.57 us
    all_to_all x1, waiting for transfers between devices, turned_blocks(): result = lax.all_to_all(result, axes[k], k, k, tiled=True)  8.41 us
    ppermute x2, starting transfers between devices, faces_of(): lax.ppermute(last, axis, up)  8.07 us
    all_to_all x1, blocking collectives, turned_blocks(): result = lax.all_to_all(result, axes[k], k, k, tiled=True)  6.05 us
    ppermute x2, waiting for transfers between devices, faces_of(): lax.ppermute(last, axis, up)  5.65 us
    ppermute x2, waiting for transfers between devices, faces_of(): lax.ppermute(leading, axis, [(b, a) for a, b in up])  4.02 us
  transfers between devices with their start and end apart: 6, of which 4 were waited for; matrix products, arithmetic and copies ran while one was open for 2% of the time, Pallas kernels for 0%

commit v1 on v0

v1 whole, which is shorter than its diff:
```python
import functools

import jax
import jax.numpy as jnp
import numpy as np
from jax import lax
from jax.experimental import pallas as pl
from jax.experimental.pallas import tpu as pltpu
from jax.sharding import PartitionSpec as P

f32, bf16 = jnp.float32, jnp.bfloat16
MESH = pl.DeviceIdType.MESH
NS, SP = 53, 56
NR, RP = 325, 336
LOG2E = 1.4426950408889634
time_step = 0.2
screen = 0.004
highest = lax.Precision.HIGHEST

def advance_kernel(species, vel_hbm, diff_hbm, mov_ref, sp, hx, ext, mv, vel_ref, diff_ref, sem_in, ss, rs, sem_out):
    rows, cols = lax.axis_size("row"), lax.axis_size("col")
    me_r, me_c = lax.axis_index("row"), lax.axis_index("col")
    above = {"row": lax.rem(me_r + 1, rows), "col": me_c}
    below = {"row": lax.rem(me_r + rows - 1, rows), "col": me_c}
    right = {"row": me_r, "col": lax.rem(me_c + 1, cols)}
    left = {"row": me_r, "col": lax.rem(me_c + cols - 1, cols)}
    barrier = pltpu.get_barrier_semaphore()
    for peer in (above, below, right, left):
        pl.semaphore_signal(barrier, inc=1, device_id=peer, device_id_type=MESH)
    loads = [pltpu.make_async_copy(species.at[:, :, pl.ds(z * 128, 128)], sp.at[z], sem_in.at[z]) for z in range(2)]
    loads += [pltpu.make_async_copy(vel_hbm, vel_ref, sem_in.at[2]), pltpu.make_async_copy(diff_hbm, diff_ref, sem_in.at[3])]
    for c in loads:
        c.start()
    pl.semaphore_wait(barrier, 4)
    x_copies = []
    for z in range(2):
        zs = pl.ds(z * 128, 128)
        x_copies.append(pltpu.make_async_remote_copy(src_ref=species.at[:, pl.ds(56, 8), zs], dst_ref=hx.at[0, z], send_sem=ss.at[2 + z], recv_sem=rs.at[2 + z], device_id=above, device_id_type=MESH))
        x_copies.append(pltpu.make_async_remote_copy(src_ref=species.at[:, pl.ds(0, 8), zs], dst_ref=hx.at[1, z], send_sem=ss.at[4 + z], recv_sem=rs.at[4 + z], device_id=below, device_id_type=MESH))
    for c in x_copies:
        c.start()
    for c in loads:
        c.wait()

    def lay(x, y):
        c = x * 8 + y
        for z in range(2):
            ext[x + 1, y + 1, :NS, z * 128:(z + 1) * 128] = sp_rows(z, c)

    def sp_rows(z, c):
        return sp.at[z].reshape(NS * 64, 128)[pl.ds(c, NS, stride=64), :]

    def lay_edge(x, _):
        lay(x, 0)
        lay(x, 7)
        return 0
    lax.fori_loop(0, 8, lay_edge, 0)
    y_up = pltpu.make_async_remote_copy(src_ref=ext.at[pl.ds(1, 8), 8], dst_ref=ext.at[pl.ds(1, 8), 0], send_sem=ss.at[0], recv_sem=rs.at[0], device_id=right, device_id_type=MESH)
    y_down = pltpu.make_async_remote_copy(src_ref=ext.at[pl.ds(1, 8), 1], dst_ref=ext.at[pl.ds(1, 8), 9], send_sem=ss.at[1], recv_sem=rs.at[1], device_id=left, device_id_type=MESH)
    y_up.start()
    y_down.start()

    def lay_inner(x, _):
        for y in range(1, 7):
            lay(x, y)
        return 0
    lax.fori_loop(0, 8, lay_inner, 0)

    own = lax.broadcasted_iota(jnp.int32, (SP, NS), 0) == lax.broadcasted_iota(jnp.int32, (SP, NS), 1)
    fifth = jnp.broadcast_to(0.2 * jnp.sum(jnp.where(own, diff_ref[...], 0.0), axis=1, keepdims=True), (SP, 256))
    lane = lax.broadcasted_iota(jnp.int32, (SP, 256), 1)
    row = lax.broadcasted_iota(jnp.int32, (SP, 256), 0)

    def move(x, y):
        c = x * 8 + y
        centre = ext[x + 1, y + 1]
        near = (ext[x, y + 1], ext[x + 2, y + 1], ext[x + 1, y], ext[x + 1, y + 2],
                jnp.where(lane == 0, centre, pltpu.roll(centre, 1, 1)), jnp.where(lane == 255, centre, pltpu.roll(centre, 255, 1)))
        speeds = [0.2 * vel_ref[d, pl.ds(c, 1), :] for d in range(3)]
        still = 1.0 - (jnp.abs(speeds[0]) + jnp.abs(speeds[1]) + jnp.abs(speeds[2]))
        total = centre * (still - 6.0 * fifth)
        for d in range(3):
            total = total + near[2 * d] * (fifth + jnp.maximum(speeds[d], 0.0))
            total = total + near[2 * d + 1] * (fifth - jnp.minimum(speeds[d], 0.0))
        total = jnp.where(row < NS, total, 2.0)
        mv[2 * c] = total[:, :128]
        mv[2 * c + 1] = total[:, 128:]

    def inner(x, _):
        def go(y, _):
            move(x, y)
            return 0
        return lax.fori_loop(1, 7, go, 0)
    lax.fori_loop(1, 7, inner, 0)
    y_up.wait()
    y_down.wait()

    @pl.when(me_c == 0)
    def _():
        ext[pl.ds(1, 8), 0] = ext[pl.ds(1, 8), 1]

    @pl.when(me_c == cols - 1)
    def _():
        ext[pl.ds(1, 8), 9] = ext[pl.ds(1, 8), 8]

    def sides(x, _):
        move(x, 0)
        move(x, 7)
        return 0
    lax.fori_loop(1, 7, sides, 0)
    middle = pltpu.make_async_copy(mv.at[pl.ds(16, 96)], mov_ref.at[pl.ds(16, 96)], sem_out.at[0])
    middle.start()
    for c in x_copies:
        c.wait()

    def lay_halo(y, _):
        for k, at in ((0, 0), (1, 9)):
            for z in range(2):
                ext[at, y + 1, :NS, z * 128:(z + 1) * 128] = hx_rows(k, z, y)
        return 0

    def hx_rows(k, z, y):
        return hx.at[k, z].reshape(NS * 8, 128)[pl.ds(y, NS, stride=8), :]
    lax.fori_loop(0, 8, lay_halo, 0)

    @pl.when(me_r == 0)
    def _():
        ext[0, pl.ds(1, 8)] = ext[1, pl.ds(1, 8)]

    @pl.when(me_r == rows - 1)
    def _():
        ext[9, pl.ds(1, 8)] = ext[8, pl.ds(1, 8)]

    def ends(y, _):
        move(0, y)
        move(7, y)
        return 0
    lax.fori_loop(0, 8, ends, 0)
    low = pltpu.make_async_copy(mv.at[pl.ds(0, 16)], mov_ref.at[pl.ds(0, 16)], sem_out.at[1])
    high = pltpu.make_async_copy(mv.at[pl.ds(112, 16)], mov_ref.at[pl.ds(112, 16)], sem_out.at[2])
    low.start()
    high.start()
    middle.wait()
    low.wait()
    high.wait()


def advance(species, velocity, diffusivity):
    hb = pl.BlockSpec(memory_space=pl.ANY)
    dma = pltpu.SemaphoreType.DMA
    return pl.pallas_call(
        advance_kernel,
        out_shape=jax.ShapeDtypeStruct((128, SP, 128), f32),
        in_specs=[hb, hb, hb],
        out_specs=hb,
        scratch_shapes=[pltpu.VMEM((2, NS, 64, 128), f32), pltpu.VMEM((2, 2, NS, 8, 128), f32), pltpu.VMEM((10, 10, SP, 256), f32), pltpu.VMEM((128, SP, 128), f32), pltpu.VMEM((3, 64, 256), f32), pltpu.VMEM((1, NS), f32),
                        dma((4,)), dma((6,)), dma((6,)), dma((3,))],
        compiler_params=pltpu.CompilerParams(collective_id=0, has_side_effects=True, vmem_limit_bytes=28 << 20),
        name="advance",
    )(species.reshape(NS, 64, 256), velocity.reshape(3, 64, 256), diffusivity[None, :])


def split3(x):
    hi = lax.reduce_precision(x, 8, 7)
    mid = lax.reduce_precision(x - hi, 8, 7)
    return hi, mid, x - hi - mid


def matrices(log_rates, reactants, products):
    rf = reactants.astype(f32)
    pf = products.astype(f32)
    bias = jnp.stack(split3(log_rates * LOG2E), axis=1)
    first = jnp.concatenate([rf, bias, rf, jnp.zeros((NR, 3), f32)], axis=1)
    first = jnp.pad(first, ((0, RP - NR), (0, 0))).astype(bf16)
    half = jnp.concatenate([jnp.pad(pf, ((0, RP - NR), (0, 3))), jnp.pad(rf, ((0, RP - NR), (0, 3)))], axis=1).T
    second = jnp.concatenate([half, half], axis=1).astype(bf16)
    return first, second


def kinetics_kernel(G, counts_ref, size_ref, mov_hbm, weight_ref, s1_ref, s2_ref, out_ref, heat_ref, mov, cur, outs, order_ref, tally_ref, sem):
    load = pltpu.make_async_copy(mov_hbm, mov, sem.at[0])
    load.start()
    for k in range(8):
        tally_ref[k] = 0

    def count(i, _):
        n = counts_ref[i]
        tally_ref[n] = tally_ref[n] + 1
        return 0
    lax.fori_loop(0, 128, count, 0)
    base = jnp.int32(0)
    for n in range(6, 0, -1):
        here = tally_ref[n]
        tally_ref[n] = base
        base = base + here

    def place(i, _):
        n = counts_ref[i]
        at = tally_ref[n]
        order_ref[at] = i
        tally_ref[n] = at + 1
        return 0
    lax.fori_loop(0, 128, place, 0)
    own = lax.broadcasted_iota(jnp.int32, (SP, NS), 0) == lax.broadcasted_iota(jnp.int32, (SP, NS), 1)
    weight = jnp.broadcast_to(jnp.sum(jnp.where(own, weight_ref[...], 0.0), axis=1, keepdims=True) / time_step, (SP, 128))
    load.wait()
    W = G * 128

    def turn(t, _):
        ids = [order_ref[t * G + j] for j in range(G)]
        ns = [counts_ref[i] for i in ids]
        for j in range(G):
            cur[:, j * 128:(j + 1) * 128] = mov[ids[j]]
        h = jnp.concatenate([jnp.full((SP, 128), size_ref[n], f32) for n in ns], axis=1)
        nb = jnp.concatenate([jnp.full((SP, 128), n, jnp.int32) for n in ns], axis=1)

        def level(k, _):
            conc = cur[...]
            lg = jnp.log2(conc)
            hi = lg.astype(bf16).astype(f32)
            xin = jnp.concatenate([hi, lg - hi], axis=0).astype(bf16)
            rates = jnp.exp2(jnp.dot(s1_ref[...], xin, preferred_element_type=f32))
            rhi = rates.astype(bf16)
            rlo = (rates - rhi.astype(f32)).astype(bf16)
            both = jnp.dot(s2_ref[...], jnp.concatenate([rhi, rlo], axis=0), preferred_element_type=f32)
            fresh = conc * (conc + h * both[:SP]) / (conc + h * both[SP:])
            cur[...] = jnp.where(nb > k, fresh, conc)
            return 0
        lax.fori_loop(0, ns[0], level, 0)
        for j in range(G):
            c, z = ids[j] // 2, ids[j] % 2
            res = cur[:, j * 128:(j + 1) * 128]
            outs[z, pl.ds(c, NS, stride=64), :] = res[:NS]
            heat_ref[z, pl.ds(c, 1), :] = jnp.sum(weight * (res - mov[ids[j]]), axis=0, keepdims=True)
        return 0
    lax.fori_loop(0, 128 // G, turn, 0)
    stores = [pltpu.make_async_copy(outs.at[z], out_ref.at[:, pl.ds(z * 128, 128)], sem.at[z]) for z in range(2)]
    for c in stores:
        c.start()
    for c in stores:
        c.wait()


def kinetics(G, moved, counts, heat_weights, first, second):
    vm = pl.BlockSpec(memory_space=pltpu.VMEM)
    sm = pl.BlockSpec(memory_space=pltpu.SMEM)
    hb = pl.BlockSpec(memory_space=pl.ANY)
    sizes = np.array([0.0] + [time_step / n for n in range(1, 8)], np.float32)
    return pl.pallas_call(
        functools.partial(kinetics_kernel, G),
        out_shape=(jax.ShapeDtypeStruct((NS * 64, 256), f32), jax.ShapeDtypeStruct((2, 64, 128), f32)),
        in_specs=[sm, sm, hb, vm, vm, vm],
        out_specs=(hb, vm),
        scratch_shapes=[
            pltpu.VMEM((128, SP, 128), f32), pltpu.VMEM((SP, G * 128), f32), pltpu.VMEM((2, NS * 64, 128), f32),
            pltpu.SMEM((128,), jnp.int32), pltpu.SMEM((8,), jnp.int32), pltpu.SemaphoreType.DMA((2,))],
        compiler_params=pltpu.CompilerParams(vmem_limit_bytes=32 << 20),
        name="kinetics",
    )(counts, jnp.asarray(sizes), moved, heat_weights[None, :], first, second)


def cosine_table(length):
    wave = np.arange(length)[:, None]
    sample = np.arange(length)[None, :] + 0.5
    weight = np.sqrt(np.where(wave == 0, 1.0, 2.0) / length)
    return (weight * np.cos(np.pi * wave * sample / length)).astype(np.float32)


def mode_values(length):
    return 2.0 - 2.0 * np.cos(np.pi * np.arange(length) / length)


def exact_dot(a, b, dims):
    return lax.dot_general(a, b, (dims, ((), ())), precision=highest, preferred_element_type=f32)


def solve_kernel(heat_ref, div_ref, tz_ref, tx_ref, ty_ref, shift_ref, ly_ref, out_ref,
                 f1, send1, recv1, yv, send2, recv2, recv3, yb, send4, recv4, fp,
                 ss1, rs1, ss2, rs2, ss3, rs3, ss4, rs4):
    rows, cols = 8, 16
    me_r, me_c = lax.axis_index("row"), lax.axis_index("col")
    barrier = pltpu.get_barrier_semaphore()
    for d in range(1, rows):
        pl.semaphore_signal(barrier, inc=1, device_id={"row": lax.rem(me_r + d, rows), "col": me_c}, device_id_type=pl.DeviceIdType.MESH)
    for d in range(1, cols):
        pl.semaphore_signal(barrier, inc=1, device_id={"row": me_r, "col": lax.rem(me_c + d, cols)}, device_id_type=pl.DeviceIdType.MESH)

    def row_copy(send, recv, ss, rs, d):
        to = lax.rem(me_r + d, rows)
        return pltpu.make_async_remote_copy(src_ref=send.at[to], dst_ref=recv.at[me_r], send_sem=ss.at[d], recv_sem=rs.at[me_r],
                                            device_id={"row": to, "col": me_c}, device_id_type=pl.DeviceIdType.MESH)

    def col_copy(send, recv, ss, rs, d):
        to = lax.rem(me_c + d, cols)
        return pltpu.make_async_remote_copy(src_ref=send.at[to], dst_ref=recv.at[me_c], send_sem=ss.at[d], recv_sem=rs.at[me_c],
                                            device_id={"row": me_r, "col": to}, device_id_type=pl.DeviceIdType.MESH)

    def row_arrival(send, recv, ss, rs, d):
        come = lax.rem(me_r + d, rows)
        return pltpu.make_async_remote_copy(src_ref=send.at[come], dst_ref=recv.at[come], send_sem=ss.at[d], recv_sem=rs.at[come],
                                            device_id={"row": come, "col": me_c}, device_id_type=pl.DeviceIdType.MESH)

    def col_arrival(send, recv, ss, rs, d):
        come = lax.rem(me_c + d, cols)
        return pltpu.make_async_remote_copy(src_ref=send.at[come], dst_ref=recv.at[come], send_sem=ss.at[d], recv_sem=rs.at[come],
                                            device_id={"row": me_r, "col": come}, device_id_type=pl.DeviceIdType.MESH)

    lane = lax.broadcasted_iota(jnp.int32, (8, 128), 1)
    part = lane // 32
    source = div_ref[...] - jnp.concatenate([heat_ref[0], heat_ref[1]], axis=1)
    forward = exact_dot(source, tz_ref[...], ((1,), (1,)))
    f1[0] = forward[:, :128]
    f1[1] = forward[:, 128:]
    for kh in range(2):
        for h in range(2):
            v = [f1[kh, pl.ds(4 * h + p, 8, stride=8), :] for p in range(4)]
            for q in range(4):
                tile = jnp.zeros((8, 128), f32)
                for p in range(4):
                    s = (p - q) * 32 % 128
                    tile = jnp.where(part == p, pltpu.roll(v[p], s, 1) if s else v[p], tile)
                send1[kh * 4 + q, :, h * 128:(h + 1) * 128] = tile
    pl.semaphore_wait(barrier, rows - 1 + cols - 1)
    sent = [row_copy(send1, recv1, ss1, rs1, d) for d in range(1, rows)]
    for c in sent:
        c.start()
    recv1[me_r] = send1[me_r]
    for d in range(1, rows):
        row_arrival(send1, recv1, ss1, rs1, d).wait_recv()
    for c in sent:
        c.wait_send()
    block = recv1[...].reshape(64, 256)
    tx = tx_ref[...]
    yv[...] = exact_dot(jnp.transpose(block), jnp.concatenate([tx, tx], axis=0), ((1,), (1,)))
    for c in range(cols):
        send2[c] = jnp.where(lane < 64, yv[pl.ds(2 * c, 8, stride=32), :], yv[pl.ds(2 * c + 1, 8, stride=32), :])
    sent = [col_copy(send2, recv2, ss2, rs2, d) for d in range(1, cols)]
    for c in sent:
        c.start()
    recv2[me_c] = send2[me_c]
    for d in range(1, cols):
        col_arrival(send2, recv2, ss2, rs2, d).wait_recv()
    for c in sent:
        c.wait_send()
    ty = ty_ref[...]
    spectrum = exact_dot(ty, recv2[...].reshape(128, 128), ((1,), (0,)))
    shift = shift_ref[pl.ds(me_r * cols + me_c, 1), :]
    spectrum = spectrum / (ly_ref[...] + shift)
    send2[...] = exact_dot(ty, spectrum, ((0,), (0,))).reshape(cols, 8, 128)
    sent = [col_copy(send2, recv3, ss3, rs3, d) for d in range(1, cols)]
    for c in sent:
        c.start()
    recv3[me_c] = send2[me_c]
    for d in range(1, cols):
        col_arrival(send2, recv3, ss3, rs3, d).wait_recv()
    for c in sent:
        c.wait_send()
    for c in range(cols):
        tile = recv3[c]
        yb[pl.ds(2 * c, 8, stride=32), :] = jnp.where(lane < 64, tile, 0.0)
        yb[pl.ds(2 * c + 1, 8, stride=32), :] = jnp.where(lane < 64, 0.0, tile)
    txt = jnp.transpose(tx)
    send4[...] = exact_dot(jnp.concatenate([txt, txt], axis=1), yb[...], ((1,), (1,))).reshape(8, 8, 256)
    sent = [row_copy(send4, recv4, ss4, rs4, d) for d in range(1, rows)]
    for c in sent:
        c.start()
    recv4[me_r] = send4[me_r]
    for d in range(1, rows):
        row_arrival(send4, recv4, ss4, rs4, d).wait_recv()
    for c in sent:
        c.wait_send()
    for kh in range(2):
        for h in range(2):
            v = [recv4[kh * 4 + q, :, h * 128:(h + 1) * 128] for q in range(4)]
            for p in range(4):
                tile = jnp.zeros((8, 128), f32)
                for q in range(4):
                    s = (q - p) * 32 % 128
                    tile = jnp.where(part == q, pltpu.roll(v[q], s, 1) if s else v[q], tile)
                fp[kh, pl.ds(4 * h + p, 8, stride=8), :] = tile
    out_ref[...] = exact_dot(jnp.concatenate([fp[0], fp[1]], axis=1), tz_ref[...], ((1,), (0,)))


def solve(heat, divergence):
    lx, ly, lz = mode_values(64), mode_values(128), mode_values(256)
    device = np.arange(128)
    lanes = np.arange(128)
    shift = screen + lx[lanes % 64][None, :] + lz[(device // 16 * 32 + device % 16 * 2)[:, None] + (lanes // 64)[None, :]]
    vm = pl.BlockSpec(memory_space=pltpu.VMEM)
    dma = pltpu.SemaphoreType.DMA
    out = pl.pallas_call(
        solve_kernel,
        out_shape=jax.ShapeDtypeStruct((64, 256), f32),
        in_specs=[vm] * 7,
        out_specs=vm,
        scratch_shapes=[
            pltpu.VMEM((2, 64, 128), f32), pltpu.VMEM((8, 8, 256), f32), pltpu.VMEM((8, 8, 256), f32), pltpu.VMEM((256, 128), f32),
            pltpu.VMEM((16, 8, 128), f32), pltpu.VMEM((16, 8, 128), f32), pltpu.VMEM((16, 8, 128), f32), pltpu.VMEM((256, 128), f32),
            pltpu.VMEM((8, 8, 256), f32), pltpu.VMEM((8, 8, 256), f32), pltpu.VMEM((2, 64, 128), f32),
            dma((8,)), dma((8,)), dma((16,)), dma((16,)), dma((16,)), dma((16,)), dma((8,)), dma((8,))],
        compiler_params=pltpu.CompilerParams(collective_id=1, has_side_effects=True, vmem_limit_bytes=16 << 20),
        name="screened_solve",
    )(heat, divergence.reshape(64, 256), jnp.asarray(cosine_table(256)), jnp.asarray(cosine_table(64)), jnp.asarray(cosine_table(128)),
      jnp.asarray(shift.astype(np.float32)), jnp.asarray(np.broadcast_to(ly[:, None], (128, 128)).astype(np.float32)))
    return out.reshape(8, 8, 256)


def local(species, velocity, diffusivity, divergence, log_rates, reactants, products, heat_weights, substeps):
    first, second = matrices(log_rates, reactants, products)
    moved = advance(species, velocity, diffusivity)
    reacted, heat = kinetics(16, moved, substeps.reshape(-1), heat_weights, first, second)
    pressure = solve(heat, divergence)
    return reacted.reshape(species.shape), pressure


def solution(mesh):
    cells = P("row", "col", None)
    fields = P(None, "row", "col", None)
    in_specs = (fields, fields, P(), cells, P(), P(), P(), P(), cells)
    return jax.shard_map(local, mesh=mesh, in_specs=in_specs, out_specs=(fields, cells), check_vma=False)
```

time: 155 us -> 107 us (0.69)
  Pallas kernels: 38.3 us -> 97.6 us
  starting transfers between devices: 58.7 us -> 0 us
  waiting for transfers between devices: 27.6 us -> 0 us
  matrix products: 8.11 us -> 0 us
  blocking collectives: 6.05 us -> 0 us
  local copies, waits for them, and re-layouts: 11 us -> 5.46 us
    pallas_call x1 -> x3, Pallas kernels: 38.3 us -> 97.6 us  [the longest x1 54.6 us: solve(): pl.pallas_call(solve_kernel, out_shape=jax.ShapeDtypeStruct((64, 256), f3...]
    all_to_all x2 -> x0, starting transfers between devices: 47.4 us -> none  [the longest x1 43.6 us: turned_blocks(): result = lax.all_to_all(result, axes[k], k, k, tiled=True)]
    all_to_all x2 -> x0, waiting for transfers between devices: 18 us -> none  [the longest x1 9.57 us: local(): lax.all_to_all(outgoing, ROW_COL, split_axis=1, concat_axis=0, tiled=True)]
    ppermute x4 -> x0, starting transfers between devices: 11.3 us -> none  [the longest x2 8.07 us: faces_of(): lax.ppermute(last, axis, up)]
    ppermute x4 -> x0, waiting for transfers between devices: 9.67 us -> none  [the longest x2 5.65 us: faces_of(): lax.ppermute(last, axis, up)]
    dot_general x6 -> x0, matrix products: 8.11 us -> none  [the longest x1 3.33 us: local(): pressure = jnp.einsum('kz,kxy->xyz', table_z, columns, precision=highest)]
    all_to_all x1 -> x0, blocking collectives: 6.05 us -> none  [turned_blocks(): result = lax.all_to_all(result, axes[k], k, k, tiled=True)]
    slice x1 -> x0, local copies, waits for them, and re-layouts: 4 us -> none  [faces_of(): leading = lax.index_in_dim(x, 0, dim, keepdims=False)]
  transfers between devices with their start and end apart: 6 -> 0, of which waited for: 4 -> 0; matrix products, arithmetic and copies ran while one was open for 2% -> 0% of each run, Pallas kernels for 0% -> 0%
where the time goes in v1:
time: 107 us
  Pallas kernels  97.6 us (91%)
  local copies, waits for them, and re-layouts  5.46 us (5%)
  other arithmetic  2.68 us (3%)
    pallas_call x1, Pallas kernels, solve(): pl.pallas_call(solve_kernel, out_shape=jax.ShapeDtypeStruct((64, 256), f3...  54.6 us
    pallas_call x1, Pallas kernels, advance(): pl.pallas_call(advance_kernel, out_shape=jax.ShapeDtypeStruct((128, SP, 1...  22 us
    pallas_call x1, Pallas kernels, kinetics(): pl.pallas_call(functools.partial(kinetics_kernel, G), out_shape=(jax.Shap...  21.1 us
    unnamed x25, local copies, waits for them, and re-layouts  5.17 us

profile of v1, /device:TPU:1, one launch (start us, length us, event | category | flops | bytes accessed | tf_op | source)
XLA Modules:
  0.0 106.6 jit_solution(4921994041152450370)
XLA Ops:
  0.6 0.7 fusion.2
  1.3 0.8 copy.19
  2.2 0.1 reshape.22.counts_ref
  2.3 0.9 convert_element_type.14
  3.2 1.0 fusion.3
  4.2 0.1 concatenate.11
  4.3 0.1 copy.21
  4.5 0.1 pad_maximum_fusion.s2_ref
  4.6 0.0 copy-start
  4.6 2.0 %copy-done = f32[53,8,8,256]{3,2,1,0:T(8,128)S(1)} copy-done((f32[53,8,8,256]{3,2,1,0:T(8,128)S(1)}, f32[53,8,8,256]{3,2,1,0:T(8,128)}, u32[]{:S(2)}) %copy-start) | copy-done | bytes 3473432
  6.6 0.0 copy-start.2
  6.6 0.9 copy-done.2
  7.5 0.0 copy-start.10
  7.5 0.7 copy-done.10
  8.1 0.0 copy-start.8
  8.1 0.0 copy-start.9
  8.1 22.0 %advance.1.mov_hbm = f32[128,56,128]{2,1,0:T(8,128)S(1)} custom-call(f32[53,64,256]{2,1,0:T(8,128)S(1)} %bitcast.9, f32[3,64,256]{2,1,0:T(8,128)S(1)} %bitcast.11, f32[1,53]{1,0:T(1,128)S(1)} %bitcast.14), custom_call_target="tpu_custom_call" | custom-call | tf_op jit(solution)/shard_map/advance/pallas_call | solution.py:151
  30.2 0.0 copy-done.8
  30.2 0.0 copy-done.9
  30.2 0.0 copy-start.1
  30.2 0.0 copy-start.3
  30.2 0.0 copy-start.4
  30.2 0.0 copy-start.5
  30.2 0.0 copy-start.6
  30.2 0.0 copy-start.7
  30.3 21.1 %kinetics.1 = (f32[3392,256]{1,0:T(8,128)}, f32[2,64,128]{2,1,0:T(8,128)S(1)}) custom-call(s32[128]{0:T(128)S(1)} %reshape.22.counts_ref, f32[8]{0:T(128)S(1)} %copy-done.9, f32[128,56,128]{2,1,0:T(8,128)S(1)} %advance.1.mov_hbm, f32[1,53]{1,0:T(1,128)S(1)} %bitcast.13, bf16[336,112]{1,0:T(8,128)(2,1)S(1)} %pad.12.clone.s1_ref, ...), custom_call_target="tpu_custom_call" | custom-call | tf_op jit(solution)/shard_map/kinetics/pallas_call | solution.py:249
  51.3 0.0 copy-done.1
  51.3 0.0 copy-done.3
  51.3 0.0 copy-done.4
  51.3 0.0 copy-done.5
  51.4 0.0 copy-done.6
  51.4 0.0 copy-done.7
  51.4 54.6 %screened_solve.1 = f32[64,256]{1,0:T(8,128)S(1)} custom-call(f32[2,64,128]{2,1,0:T(8,128)S(1)} %get-tuple-element.5.heat_ref, f32[64,256]{1,0:T(8,128)S(1)} %bitcast.12, f32[256,256]{1,0:T(8,128)S(1)} %copy-done.1, f32[64,64]{1,0:T(8,128)S(1)} %copy-done.7, f32[128,128]{1,0:T(8,128)S(1)} %copy-done.6, f32[128,128]{1,0:T(8,128)S(1)} %copy-done.5, ...), custom_call_target="tpu_custom_call" | custom-call | tf_op jit(solution)/shard_map/screened_solve/pallas_call | solution.py:391
  106.0 0.6 copy.23
  (6 shorter events, 0.1 us)
Async XLA Ops:
  4.6 2.0 %copy-start = (f32[53,8,8,256]{3,2,1,0:T(8,128)S(1)}, f32[53,8,8,256]{3,2,1,0:T(8,128)}, u32[]{:S(2)}) copy-start(f32[53,8,8,256]{3,2,1,0:T(8,128)} %param.15) | copy-start | bytes 10420228
  6.6 0.9 copy-start.2
  7.5 0.7 copy-start.10
  8.1 22.0 %copy-start.8 = (f32[53]{0:T(128)S(1)}, f32[53]{0:T(128)}, u32[]{:S(2)}) copy-start(f32[53]{0:T(128)} %param.22) | copy-start | bytes 640
  8.1 22.0 %copy-start.9 = (f32[8]{0:T(128)S(1)}, f32[8]{0:T(128)}, u32[]{:S(2)}) copy-start(f32[8]{0:T(128)} %constant.20.clone.size_ref) | copy-start | bytes 100
  30.2 21.1 %copy-start.1 = (f32[256,256]{1,0:T(8,128)S(1)}, f32[256,256]{1,0:T(8,128)}, u32[]{:S(2)}) copy-start(f32[256,256]{1,0:T(8,128)} %constant.21.clone.tz_ref) | copy-start | bytes 786436
  30.2 21.1 %copy-start.3 = (f32[8,8,256]{2,1,0:T(8,128)S(1)}, f32[8,8,256]{2,1,0:T(8,128)}, u32[]{:S(2)}) copy-start(f32[8,8,256]{2,1,0:T(8,128)} %param.18) | copy-start | bytes 196612
  30.2 21.1 %copy-start.4 = (f32[128,128]{1,0:T(8,128)S(1)}, f32[128,128]{1,0:T(8,128)}, u32[]{:S(2)}) copy-start(f32[128,128]{1,0:T(8,128)} %constant.25.clone.ly_ref) | copy-start | bytes 196612
  30.2 21.1 %copy-start.5 = (f32[128,128]{1,0:T(8,128)S(1)}, f32[128,128]{1,0:T(8,128)}, u32[]{:S(2)}) copy-start(f32[128,128]{1,0:T(8,128)} %constant.24.clone.shift_ref) | copy-start | bytes 196612
  30.2 21.1 %copy-start.6 = (f32[128,128]{1,0:T(8,128)S(1)}, f32[128,128]{1,0:T(8,128)}, u32[]{:S(2)}) copy-start(f32[128,128]{1,0:T(8,128)} %constant.23.clone.ty_ref) | copy-start | bytes 196612
  30.2 21.1 %copy-start.7 = (f32[64,64]{1,0:T(8,128)S(1)}, f32[64,64]{1,0:T(8,128)}, u32[]{:S(2)}) copy-start(f32[64,64]{1,0:T(8,128)} %constant.22.clone.tx_ref) | copy-start | bytes 49156

commit v2 on v1

--- a/solution.py
+++ b/solution.py
@@ -17,7 +17,42 @@
 screen = 0.004
 highest = lax.Precision.HIGHEST
 
-def advance_kernel(species, vel_hbm, diff_hbm, mov_ref, sp, hx, ext, mv, vel_ref, diff_ref, sem_in, ss, rs, sem_out):
+def split3(x):
+    hi = x.astype(bf16).astype(f32)
+    mid = (x - hi).astype(bf16).astype(f32)
+    return hi, mid, x - hi - mid
+
+
+def build_matrices(log_rates, react_ref, prod_ref, react, prod, first_ref, second_ref):
+    react[...] = jnp.zeros_like(react)
+    prod[...] = jnp.zeros_like(prod)
+    react[:NR, :NS] = react_ref[...].astype(f32)
+    prod[:NR, :NS] = prod_ref[...].astype(f32)
+    rp = react[...]
+    own = lax.broadcasted_iota(jnp.int32, (RP, NR), 0) == lax.broadcasted_iota(jnp.int32, (RP, NR), 1)
+    hi, mid, low = split3(jnp.sum(jnp.where(own, log_rates[...], 0.0), axis=1, keepdims=True) * LOG2E)
+    lane = lax.broadcasted_iota(jnp.int32, (RP, 128), 1)
+    later = pltpu.roll(rp, SP, 1)
+    both = jnp.where(lane == NS, hi, jnp.where(lane == NS + 1, mid, jnp.where(lane == NS + 2, low, rp + later)))
+    first_ref[...] = both[:, :2 * SP].astype(bf16)
+    outcome = prod[...] + later
+    second_ref[...] = jnp.transpose(jnp.concatenate([outcome, outcome], axis=0))[:2 * SP].astype(bf16)
+
+
+def build_order(counts, order_ref):
+    n = counts[...].astype(f32)
+    row = lax.broadcasted_iota(jnp.int32, (128, 128), 0)
+    lane = lax.broadcasted_iota(jnp.int32, (128, 128), 1)
+    column = jnp.sum(jnp.where(row == lane, n, 0.0), axis=1, keepdims=True)
+    ahead = jnp.where(n > column, 1.0, jnp.where(n == column, jnp.where(lane < row, 1.0, 0.0), 0.0))
+    rank = jnp.sum(ahead, axis=1, keepdims=True).astype(jnp.int32)
+    here = rank == lane
+    order_ref[0:1, :] = jnp.sum(jnp.where(here, row.astype(f32), 0.0), axis=0, keepdims=True).astype(jnp.int32)
+    order_ref[1:2, :] = jnp.sum(jnp.where(here, jnp.broadcast_to(column, (128, 128)), 0.0), axis=0, keepdims=True).astype(jnp.int32)
+
+
+def advance_kernel(species, vel_hbm, diff_hbm, rates_hbm, react_hbm, prod_hbm, counts_hbm, mov_ref, first_ref, second_ref, order_ref,
+                   sp, hx, ext, mv, vel_ref, diff_ref, rates_ref, react_ref, prod_ref, counts_ref, react, prod, sem_in, ss, rs, sem_out):
     rows, cols = lax.axis_size("row"), lax.axis_size("col")
     me_r, me_c = lax.axis_index("row"), lax.axis_index("col")
     above = {"row": lax.rem(me_r + 1, rows), "col": me_c}
@@ -29,7 +64,8 @@
         pl.semaphore_signal(barrier, inc=1, device_id=peer, device_id_type=MESH)
     loads = [pltpu.make_async_copy(species.at[:, :, pl.ds(z * 128, 128)], sp.at[z], sem_in.at[z]) for z in range(2)]
     loads += [pltpu.make_async_copy(vel_hbm, vel_ref, sem_in.at[2]), pltpu.make_async_copy(diff_hbm, diff_ref, sem_in.at[3])]
-    for c in loads:
+    extra = [pltpu.make_async_copy(a, b, sem_in.at[4 + k]) for k, (a, b) in enumerate(((rates_hbm, rates_ref), (react_hbm, react_ref), (prod_hbm, prod_ref), (counts_hbm, counts_ref)))]
+    for c in loads + extra:
         c.start()
     pl.semaphore_wait(barrier, 4)
     x_copies = []
@@ -92,6 +128,10 @@
             return 0
         return lax.fori_loop(1, 7, go, 0)
     lax.fori_loop(1, 7, inner, 0)
+    for c in extra:
+        c.wait()
+    build_matrices(rates_ref, react_ref, prod_ref, react, prod, first_ref, second_ref)
+    build_order(counts_ref, order_ref)
     y_up.wait()
     y_down.wait()
 
@@ -145,72 +185,53 @@
     high.wait()
 
 
-def advance(species, velocity, diffusivity):
+def advance(species, velocity, diffusivity, log_rates, reactants, products, counts):
+    vm = pl.BlockSpec(memory_space=pltpu.VMEM)
     hb = pl.BlockSpec(memory_space=pl.ANY)
     dma = pltpu.SemaphoreType.DMA
+    shape = jax.ShapeDtypeStruct
     return pl.pallas_call(
         advance_kernel,
-        out_shape=jax.ShapeDtypeStruct((128, SP, 128), f32),
-        in_specs=[hb, hb, hb],
-        out_specs=hb,
-        scratch_shapes=[pltpu.VMEM((2, NS, 64, 128), f32), pltpu.VMEM((2, 2, NS, 8, 128), f32), pltpu.VMEM((10, 10, SP, 256), f32), pltpu.VMEM((128, SP, 128), f32), pltpu.VMEM((3, 64, 256), f32), pltpu.VMEM((1, NS), f32),
-                        dma((4,)), dma((6,)), dma((6,)), dma((3,))],
-        compiler_params=pltpu.CompilerParams(collective_id=0, has_side_effects=True, vmem_limit_bytes=28 << 20),
+        out_shape=(shape((128, SP, 128), f32), shape((RP, 2 * SP), bf16), shape((2 * SP, 2 * RP), bf16), shape((2, 128), jnp.int32)),
+        in_specs=[hb] * 7,
+        out_specs=(hb, vm, vm, vm),
+        scratch_shapes=[pltpu.VMEM((2, NS, 64, 128), f32), pltpu.VMEM((2, 2, NS, 8, 128), f32), pltpu.VMEM((10, 10, SP, 256), f32), pltpu.VMEM((128, SP, 128), f32),
+                        pltpu.VMEM((3, 64, 256), f32), pltpu.VMEM((1, NS), f32), pltpu.VMEM((1, NR), f32), pltpu.VMEM((NR, NS), jnp.int32), pltpu.VMEM((NR, NS), jnp.int32),
+                        pltpu.VMEM((1, 128), jnp.int32), pltpu.VMEM((RP, 128), f32), pltpu.VMEM((RP, 128), f32), dma((8,)), dma((6,)), dma((6,)), dma((3,))],
+        compiler_params=pltpu.CompilerParams(collective_id=0, has_side_effects=True, vmem_limit_bytes=60 << 20),
         name="advance",
-    )(species.reshape(NS, 64, 256), velocity.reshape(3, 64, 256), diffusivity[None, :])
-
-
-def split3(x):
-    hi = lax.reduce_precision(x, 8, 7)
-    mid = lax.reduce_precision(x - hi, 8, 7)
-    return hi, mid, x - hi - mid
-
-
-def matrices(log_rates, reactants, products):
-    rf = reactants.astype(f32)
-    pf = products.astype(f32)
-    bias = jnp.stack(split3(log_rates * LOG2E), axis=1)
-    first = jnp.concatenate([rf, bias, rf, jnp.zeros((NR, 3), f32)], axis=1)
-    first = jnp.pad(first, ((0, RP - NR), (0, 0))).astype(bf16)
-    half = jnp.concatenate([jnp.pad(pf, ((0, RP - NR), (0, 3))), jnp.pad(rf, ((0, RP - NR), (0, 3)))], axis=1).T
-    second = jnp.concatenate([half, half], axis=1).astype(bf16)
-    return first, second
-
-
-def kinetics_kernel(G, counts_ref, size_ref, mov_hbm, weight_ref, s1_ref, s2_ref, out_ref, heat_ref, mov, cur, outs, order_ref, tally_ref, sem):
-    load = pltpu.make_async_copy(mov_hbm, mov, sem.at[0])
-    load.start()
-    for k in range(8):
-        tally_ref[k] = 0
-
-    def count(i, _):
-        n = counts_ref[i]
-        tally_ref[n] = tally_ref[n] + 1
-        return 0
-    lax.fori_loop(0, 128, count, 0)
-    base = jnp.int32(0)
-    for n in range(6, 0, -1):
-        here = tally_ref[n]
-        tally_ref[n] = base
-        base = base + here
-
-    def place(i, _):
-        n = counts_ref[i]
-        at = tally_ref[n]
-        order_ref[at] = i
-        tally_ref[n] = at + 1
-        return 0
-    lax.fori_loop(0, 128, place, 0)
+    )(species.reshape(NS, 64, 256), velocity.reshape(3, 64, 256), diffusivity[None, :], log_rates[None, :], reactants, products, counts[None, :])
+
+
+def kinetics_kernel(G, order_ref, size_ref, mov_hbm, weight_hbm, s1_hbm, s2_hbm, out_ref, heat_ref, mov, cur, outs, weight_ref, s1_ref, s2_ref, sem, arrive):
+    turns = 128 // G
+
+    def fetch(t, slot):
+        return [pltpu.make_async_copy(mov_hbm.at[order_ref[0, t * G + j]], mov.at[slot, j], arrive.at[slot]) for j in range(G)]
+    for c in fetch(0, 0):
+        c.start()
+    constants = [pltpu.make_async_copy(a, b, sem.at[k]) for k, (a, b) in enumerate(((weight_hbm, weight_ref), (s1_hbm, s1_ref), (s2_hbm, s2_ref)))]
+    for c in constants:
+        c.start()
+    for c in constants:
+        c.wait()
     own = lax.broadcasted_iota(jnp.int32, (SP, NS), 0) == lax.broadcasted_iota(jnp.int32, (SP, NS), 1)
     weight = jnp.broadcast_to(jnp.sum(jnp.where(own, weight_ref[...], 0.0), axis=1, keepdims=True) / time_step, (SP, 128))
-    load.wait()
     W = G * 128
 
     def turn(t, _):
-        ids = [order_ref[t * G + j] for j in range(G)]
-        ns = [counts_ref[i] for i in ids]
+        slot = t % 2
+
+        @pl.when(t + 1 < turns)
+        def _():
+            for c in fetch(t + 1, 1 - slot):
+                c.start()
+        ids = [order_ref[0, t * G + j] for j in range(G)]
+        ns = [order_ref[1, t * G + j] for j in range(G)]
+        for c in fetch(t, slot):
+            c.wait()
         for j in range(G):
-            cur[:, j * 128:(j + 1) * 128] = mov[ids[j]]
+            cur[:, j * 128:(j + 1) * 128] = mov[slot, j]
         h = jnp.concatenate([jnp.full((SP, 128), size_ref[n], f32) for n in ns], axis=1)
         nb = jnp.concatenate([jnp.full((SP, 128), n, jnp.int32) for n in ns], axis=1)
 
@@ -231,9 +252,9 @@
             c, z = ids[j] // 2, ids[j] % 2
             res = cur[:, j * 128:(j + 1) * 128]
             outs[z, pl.ds(c, NS, stride=64), :] = res[:NS]
-            heat_ref[z, pl.ds(c, 1), :] = jnp.sum(weight * (res - mov[ids[j]]), axis=0, keepdims=True)
-        return 0
-    lax.fori_loop(0, 128 // G, turn, 0)
+            heat_ref[z, pl.ds(c, 1), :] = jnp.sum(weight * (res - mov[slot, j]), axis=0, keepdims=True)
+        return 0
+    lax.fori_loop(0, turns, turn, 0)
     stores = [pltpu.make_async_copy(outs.at[z], out_ref.at[:, pl.ds(z * 128, 128)], sem.at[z]) for z in range(2)]
     for c in stores:
         c.start()
@@ -241,7 +262,7 @@
         c.wait()
 
 
-def kinetics(G, moved, counts, heat_weights, first, second):
+def kinetics(G, moved, order, heat_weights, first, second):
     vm = pl.BlockSpec(memory_space=pltpu.VMEM)
     sm = pl.BlockSpec(memory_space=pltpu.SMEM)
     hb = pl.BlockSpec(memory_space=pl.ANY)
@@ -249,14 +270,14 @@
     return pl.pallas_call(
         functools.partial(kinetics_kernel, G),
         out_shape=(jax.ShapeDtypeStruct((NS * 64, 256), f32), jax.ShapeDtypeStruct((2, 64, 128), f32)),
-        in_specs=[sm, sm, hb, vm, vm, vm],
+        in_specs=[sm, sm, hb, hb, hb, hb],
         out_specs=(hb, vm),
         scratch_shapes=[
-            pltpu.VMEM((128, SP, 128), f32), pltpu.VMEM((SP, G * 128), f32), pltpu.VMEM((2, NS * 64, 128), f32),
-            pltpu.SMEM((128,), jnp.int32), pltpu.SMEM((8,), jnp.int32), pltpu.SemaphoreType.DMA((2,))],
-        compiler_params=pltpu.CompilerParams(vmem_limit_bytes=32 << 20),
+            pltpu.VMEM((2, G, SP, 128), f32), pltpu.VMEM((SP, G * 128), f32), pltpu.VMEM((2, NS * 64, 128), f32), pltpu.VMEM((1, NS), f32),
+            pltpu.VMEM((RP, 2 * SP), bf16), pltpu.VMEM((2 * SP, 2 * RP), bf16), pltpu.SemaphoreType.DMA((3,)), pltpu.SemaphoreType.DMA((2,))],
+        compiler_params=pltpu.CompilerParams(vmem_limit_bytes=60 << 20),
         name="kinetics",
-    )(counts, jnp.asarray(sizes), moved, heat_weights[None, :], first, second)
+    )(order, jnp.asarray(sizes), moved, heat_weights[None, :], first, second)
 
 
 def cosine_table(length):
@@ -274,11 +295,16 @@
     return lax.dot_general(a, b, (dims, ((), ())), precision=highest, preferred_element_type=f32)
 
 
-def solve_kernel(heat_ref, div_ref, tz_ref, tx_ref, ty_ref, shift_ref, ly_ref, out_ref,
+def solve_kernel(heat_hbm, div_hbm, tz_hbm, tx_hbm, ty_hbm, shift_hbm, ly_hbm, out_ref,
+                 heat_ref, div_ref, tz_ref, tx_ref, ty_ref, shift_ref, ly_ref, sem_in,
                  f1, send1, recv1, yv, send2, recv2, recv3, yb, send4, recv4, fp,
                  ss1, rs1, ss2, rs2, ss3, rs3, ss4, rs4):
     rows, cols = 8, 16
     me_r, me_c = lax.axis_index("row"), lax.axis_index("col")
+    pairs = ((heat_hbm, heat_ref), (div_hbm, div_ref), (tz_hbm, tz_ref), (tx_hbm, tx_ref), (ty_hbm, ty_ref), (shift_hbm, shift_ref), (ly_hbm, ly_ref))
+    loads = [pltpu.make_async_copy(a, b, sem_in.at[k]) for k, (a, b) in enumerate(pairs)]
+    for c in loads:
+        c.start()
     barrier = pltpu.get_barrier_semaphore()
     for d in range(1, rows):
         pl.semaphore_signal(barrier, inc=1, device_id={"row": lax.rem(me_r + d, rows), "col": me_c}, device_id_type=pl.DeviceIdType.MESH)
@@ -307,6 +333,8 @@
 
     lane = lax.broadcasted_iota(jnp.int32, (8, 128), 1)
     part = lane // 32
+    for c in loads:
+        c.wait()
     source = div_ref[...] - jnp.concatenate([heat_ref[0], heat_ref[1]], axis=1)
     forward = exact_dot(source, tz_ref[...], ((1,), (1,)))
     f1[0] = forward[:, :128]
@@ -387,18 +415,21 @@
     lanes = np.arange(128)
     shift = screen + lx[lanes % 64][None, :] + lz[(device // 16 * 32 + device % 16 * 2)[:, None] + (lanes // 64)[None, :]]
     vm = pl.BlockSpec(memory_space=pltpu.VMEM)
+    hb = pl.BlockSpec(memory_space=pl.ANY)
     dma = pltpu.SemaphoreType.DMA
     out = pl.pallas_call(
         solve_kernel,
         out_shape=jax.ShapeDtypeStruct((64, 256), f32),
-        in_specs=[vm] * 7,
+        in_specs=[hb] * 7,
         out_specs=vm,
         scratch_shapes=[
+            pltpu.VMEM((2, 64, 128), f32), pltpu.VMEM((64, 256), f32), pltpu.VMEM((256, 256), f32), pltpu.VMEM((64, 64), f32), pltpu.VMEM((128, 128), f32),
+            pltpu.VMEM((128, 128), f32), pltpu.VMEM((128, 128), f32), dma((7,)),
             pltpu.VMEM((2, 64, 128), f32), pltpu.VMEM((8, 8, 256), f32), pltpu.VMEM((8, 8, 256), f32), pltpu.VMEM((256, 128), f32),
             pltpu.VMEM((16, 8, 128), f32), pltpu.VMEM((16, 8, 128), f32), pltpu.VMEM((16, 8, 128), f32), pltpu.VMEM((256, 128), f32),
             pltpu.VMEM((8, 8, 256), f32), pltpu.VMEM((8, 8, 256), f32), pltpu.VMEM((2, 64, 128), f32),
             dma((8,)), dma((8,)), dma((16,)), dma((16,)), dma((16,)), dma((16,)), dma((8,)), dma((8,))],
-        compiler_params=pltpu.CompilerParams(collective_id=1, has_side_effects=True, vmem_limit_bytes=16 << 20),
+        compiler_params=pltpu.CompilerParams(collective_id=1, has_side_effects=True, vmem_limit_bytes=60 << 20),
         name="screened_solve",
     )(heat, divergence.reshape(64, 256), jnp.asarray(cosine_table(256)), jnp.asarray(cosine_table(64)), jnp.asarray(cosine_table(128)),
       jnp.asarray(shift.astype(np.float32)), jnp.asarray(np.broadcast_to(ly[:, None], (128, 128)).astype(np.float32)))
@@ -406,9 +437,8 @@
 
 
 def local(species, velocity, diffusivity, divergence, log_rates, reactants, products, heat_weights, substeps):
-    first, second = matrices(log_rates, reactants, products)
-    moved = advance(species, velocity, diffusivity)
-    reacted, heat = kinetics(16, moved, substeps.reshape(-1), heat_weights, first, second)
+    moved, first, second, order = advance(species, velocity, diffusivity, log_rates, reactants, products, substeps.reshape(-1))
+    reacted, heat = kinetics(16, moved, order, heat_weights, first, second)
     pressure = solve(heat, divergence)
     return reacted.reshape(species.shape), pressure
 

time: 107 us -> 109 us (1.019)
  other arithmetic: 2.68 us -> 0 us
  Pallas kernels: 97.6 us -> 100 us
  local copies, waits for them, and re-layouts: 5.46 us -> 7.53 us
    convert_element_type x2 -> x0, other arithmetic: 1.88 us -> none  [the longest x1 0.98 us: matrices(): rf = reactants.astype(f32)]
    pallas_call x1, Pallas kernels: 22 us -> 23.3 us  [advance(): pl.pallas_call(advance_kernel, out_shape=(shape((128, SP, 128), f32), sha...]
    broadcast_in_dim x1, local copies, waits for them, and re-layouts: 0.01 us -> 1.25 us  [advance(): log_rates[None, :]]
    unnamed x25 -> x4, local copies, waits for them, and re-layouts: 5.17 us -> 5.63 us
where the time goes in v2:
time: 109 us; the launch traced here: 108 us
  Pallas kernels  100 us (92%)
  local copies, waits for them, and re-layouts  7.53 us (7%)
    pallas_call x1, Pallas kernels, solve(): pl.pallas_call(solve_kernel, out_shape=jax.ShapeDtypeStruct((64, 256), f3...  55.1 us
    pallas_call x1, Pallas kernels, advance(): pl.pallas_call(advance_kernel, out_shape=(shape((128, SP, 128), f32), sha...  23.3 us
    pallas_call x1, Pallas kernels, kinetics(): pl.pallas_call(functools.partial(kinetics_kernel, G), out_shape=(jax.Shap...  21.6 us
    unnamed x4, local copies, waits for them, and re-layouts  5.63 us

profile of v2, /device:TPU:1, one launch (start us, length us, event | category | flops | bytes accessed | tf_op | source)
XLA Modules:
  0.0 108.2 jit_solution(13670887427927275999)
XLA Ops:
  0.6 1.2 %broadcast_in_dim.10.rates_hbm = f32[1,325]{1,0:T(1,128)} reshape(f32[325]{0:T(512)} %param.19) | data formatting | bytes 2600 | tf_op jit(solution)/shard_map/broadcast_in_dim | solution.py:203
  1.9 0.8 copy.20
  2.7 0.7 broadcast_in_dim_reshape.3.counts_hbm
  3.3 1.7 %copy.21.react_hbm = s32[325,53]{1,0:T(8,128)} copy(s32[325,53]{0,1:T(8,128)} %param.20) | data formatting | bytes 137800 | tf_op args[5]
  5.0 1.7 %copy.22.prod_hbm = s32[325,53]{1,0:T(8,128)} copy(s32[325,53]{0,1:T(8,128)} %param.21) | data formatting | bytes 137800 | tf_op args[6]
  6.7 23.3 %advance.1 = (f32[128,56,128]{2,1,0:T(8,128)}, bf16[336,112]{1,0:T(8,128)(2,1)}, bf16[112,672]{1,0:T(8,128)(2,1)}, s32[2,128]{1,0:T(2,128)}) custom-call(f32[53,64,256]{2,1,0:T(8,128)} %bitcast.7, f32[3,64,256]{2,1,0:T(8,128)} %bitcast.9, f32[1,53]{1,0:T(1,128)} %bitcast.12, f32[1,325]{1,0:T(1,128)} %broadcast_in_dim.10.rates_hbm, ...), custom_call_target="tpu_custom_call" | custom-call | tf_op jit(solution)/shard_map/advance/pallas_call | solution.py:193
  30.0 21.6 %kinetics.1 = (f32[3392,256]{1,0:T(8,128)}, f32[2,64,128]{2,1,0:T(8,128)}) custom-call(s32[2,128]{1,0:T(2,128)} %get-tuple-element.8.order_ref, f32[8]{0:T(128)} %constant.12.clone.size_ref, f32[128,56,128]{2,1,0:T(8,128)} %get-tuple-element.9.mov_hbm, f32[1,53]{1,0:T(1,128)} %bitcast.11, bf16[336,112]{1,0:T(8,128)(2,1)} %get-tuple-element.10.s1_hbm, ...), custom_call_target="tpu_custom_call" | custom-call | tf_op jit(solution)/shard_map/kinetics/pallas_call | solution.py:270
  51.6 55.1 %screened_solve.1 = f32[64,256]{1,0:T(8,128)} custom-call(f32[2,64,128]{2,1,0:T(8,128)} %get-tuple-element.13.heat_hbm, f32[64,256]{1,0:T(8,128)} %bitcast.10, f32[256,256]{1,0:T(8,128)} %constant.13.clone.tz_hbm, f32[64,64]{1,0:T(8,128)} %constant.14.clone.tx_hbm, f32[128,128]{1,0:T(8,128)} %constant.15.clone.ty_hbm, f32[128,128]{1,0:T(8,128)} %constant.16.clone.shift_hbm, ...), custom_call_target="tpu_custom_call" | custom-call | tf_op jit(solution)/shard_map/screened_solve/pallas_call | solution.py:420
  106.8 1.5 %copy.24 = f32[8,8,256]{2,1,0:T(8,128)} copy(f32[8,8,256]{2,1,0:T(8,128)} %bitcast.8) | data formatting | bytes 131072

commit v3 on v2

--- a/solution.py
+++ b/solution.py
@@ -23,27 +23,33 @@
     return hi, mid, x - hi - mid
 
 
-def build_matrices(log_rates, react_ref, prod_ref, react, prod, first_ref, second_ref):
+def build_matrices(log_rates, react_ref, prod_ref, react, prod, halves, first_ref, second_ref):
     react[...] = jnp.zeros_like(react)
     prod[...] = jnp.zeros_like(prod)
-    react[:NR, :NS] = react_ref[...].astype(f32)
-    prod[:NR, :NS] = prod_ref[...].astype(f32)
-    rp = react[...]
+    react[:NS, :NR] = react_ref[...].astype(f32)
+    prod[:NS, :NR] = prod_ref[...].astype(f32)
+    rt, pt = react[...], prod[...]
+    rp = jnp.transpose(rt)[:RP]
     own = lax.broadcasted_iota(jnp.int32, (RP, NR), 0) == lax.broadcasted_iota(jnp.int32, (RP, NR), 1)
-    hi, mid, low = split3(jnp.sum(jnp.where(own, log_rates[...], 0.0), axis=1, keepdims=True) * LOG2E)
+    hi, mid, low = split3(jnp.sum(jnp.where(own, log_rates[...].reshape(1, NR), 0.0), axis=1, keepdims=True) * LOG2E)
     lane = lax.broadcasted_iota(jnp.int32, (RP, 128), 1)
     later = pltpu.roll(rp, SP, 1)
     both = jnp.where(lane == NS, hi, jnp.where(lane == NS + 1, mid, jnp.where(lane == NS + 2, low, rp + later)))
     first_ref[...] = both[:, :2 * SP].astype(bf16)
-    outcome = prod[...] + later
-    second_ref[...] = jnp.transpose(jnp.concatenate([outcome, outcome], axis=0))[:2 * SP].astype(bf16)
+    outcome = jnp.concatenate([pt[:SP], rt[:SP]], axis=0)
+    halves[:, :384] = outcome
+    halves[:, RP:RP + 384] = outcome
+    second_ref[...] = halves[:, :2 * RP].astype(bf16)
 
 
 def build_order(counts, order_ref):
-    n = counts[...].astype(f32)
     row = lax.broadcasted_iota(jnp.int32, (128, 128), 0)
     lane = lax.broadcasted_iota(jnp.int32, (128, 128), 1)
-    column = jnp.sum(jnp.where(row == lane, n, 0.0), axis=1, keepdims=True)
+    given = jnp.concatenate([counts[:, z, :] for z in range(2)], axis=0).astype(f32)
+    tall = jnp.dot((lax.broadcasted_iota(jnp.int32, (128, 16), 0) // 8 == lax.broadcasted_iota(jnp.int32, (128, 16), 1)).astype(f32), given, preferred_element_type=f32)
+    mine = lax.broadcasted_iota(jnp.int32, (128, 8), 0) % 8 == lax.broadcasted_iota(jnp.int32, (128, 8), 1)
+    column = jnp.sum(jnp.where(mine, tall, 0.0), axis=1, keepdims=True)
+    n = jnp.sum(jnp.where(row == lane, column, 0.0), axis=0, keepdims=True)
     ahead = jnp.where(n > column, 1.0, jnp.where(n == column, jnp.where(lane < row, 1.0, 0.0), 0.0))
     rank = jnp.sum(ahead, axis=1, keepdims=True).astype(jnp.int32)
     here = rank == lane
@@ -52,7 +58,7 @@
 
 
 def advance_kernel(species, vel_hbm, diff_hbm, rates_hbm, react_hbm, prod_hbm, counts_hbm, mov_ref, first_ref, second_ref, order_ref,
-                   sp, hx, ext, mv, vel_ref, diff_ref, rates_ref, react_ref, prod_ref, counts_ref, react, prod, sem_in, ss, rs, sem_out):
+                   sp, hx, ext, mv, vel_ref, diff_ref, rates_ref, react_ref, prod_ref, counts_ref, react, prod, halves, sem_in, ss, rs, sem_out):
     rows, cols = lax.axis_size("row"), lax.axis_size("col")
     me_r, me_c = lax.axis_index("row"), lax.axis_index("col")
     above = {"row": lax.rem(me_r + 1, rows), "col": me_c}
@@ -119,8 +125,8 @@
             total = total + near[2 * d] * (fifth + jnp.maximum(speeds[d], 0.0))
             total = total + near[2 * d + 1] * (fifth - jnp.minimum(speeds[d], 0.0))
         total = jnp.where(row < NS, total, 2.0)
-        mv[2 * c] = total[:, :128]
-        mv[2 * c + 1] = total[:, 128:]
+        mv[c] = total[:, :128]
+        mv[64 + c] = total[:, 128:]
 
     def inner(x, _):
         def go(y, _):
@@ -130,7 +136,7 @@
     lax.fori_loop(1, 7, inner, 0)
     for c in extra:
         c.wait()
-    build_matrices(rates_ref, react_ref, prod_ref, react, prod, first_ref, second_ref)
+    build_matrices(rates_ref, react_ref, prod_ref, react, prod, halves, first_ref, second_ref)
     build_order(counts_ref, order_ref)
     y_up.wait()
     y_down.wait()
@@ -148,8 +154,9 @@
         move(x, 7)
         return 0
     lax.fori_loop(1, 7, sides, 0)
-    middle = pltpu.make_async_copy(mv.at[pl.ds(16, 96)], mov_ref.at[pl.ds(16, 96)], sem_out.at[0])
-    middle.start()
+    middle = [pltpu.make_async_copy(mv.at[pl.ds(64 * z + 8, 48)], mov_ref.at[pl.ds(64 * z + 8, 48)], sem_out.at[z]) for z in range(2)]
+    for c in middle:
+        c.start()
     for c in x_copies:
         c.wait()
 
@@ -176,16 +183,14 @@
         move(7, y)
         return 0
     lax.fori_loop(0, 8, ends, 0)
-    low = pltpu.make_async_copy(mv.at[pl.ds(0, 16)], mov_ref.at[pl.ds(0, 16)], sem_out.at[1])
-    high = pltpu.make_async_copy(mv.at[pl.ds(112, 16)], mov_ref.at[pl.ds(112, 16)], sem_out.at[2])
-    low.start()
-    high.start()
-    middle.wait()
-    low.wait()
-    high.wait()
-
-
-def advance(species, velocity, diffusivity, log_rates, reactants, products, counts):
+    outer = [pltpu.make_async_copy(mv.at[pl.ds(at, 8)], mov_ref.at[pl.ds(at, 8)], sem_out.at[2 + k]) for k, at in enumerate((0, 56, 64, 120))]
+    for c in outer:
+        c.start()
+    for c in middle + outer:
+        c.wait()
+
+
+def advance(species, velocity, diffusivity, log_rates, reactants, products, substeps):
     vm = pl.BlockSpec(memory_space=pltpu.VMEM)
     hb = pl.BlockSpec(memory_space=pl.ANY)
     dma = pltpu.SemaphoreType.DMA
@@ -196,11 +201,11 @@
         in_specs=[hb] * 7,
         out_specs=(hb, vm, vm, vm),
         scratch_shapes=[pltpu.VMEM((2, NS, 64, 128), f32), pltpu.VMEM((2, 2, NS, 8, 128), f32), pltpu.VMEM((10, 10, SP, 256), f32), pltpu.VMEM((128, SP, 128), f32),
-                        pltpu.VMEM((3, 64, 256), f32), pltpu.VMEM((1, NS), f32), pltpu.VMEM((1, NR), f32), pltpu.VMEM((NR, NS), jnp.int32), pltpu.VMEM((NR, NS), jnp.int32),
-                        pltpu.VMEM((1, 128), jnp.int32), pltpu.VMEM((RP, 128), f32), pltpu.VMEM((RP, 128), f32), dma((8,)), dma((6,)), dma((6,)), dma((3,))],
+                        pltpu.VMEM((3, 64, 256), f32), pltpu.VMEM((1, NS), f32), pltpu.VMEM((NR,), f32), pltpu.VMEM((NS, NR), jnp.int32), pltpu.VMEM((NS, NR), jnp.int32),
+                        pltpu.VMEM((8, 2, 8), jnp.int32), pltpu.VMEM((128, 384), f32), pltpu.VMEM((128, 384), f32), pltpu.VMEM((2 * SP, RP + 384), f32), dma((8,)), dma((6,)), dma((6,)), dma((6,))],
         compiler_params=pltpu.CompilerParams(collective_id=0, has_side_effects=True, vmem_limit_bytes=60 << 20),
         name="advance",
-    )(species.reshape(NS, 64, 256), velocity.reshape(3, 64, 256), diffusivity[None, :], log_rates[None, :], reactants, products, counts[None, :])
+    )(species.reshape(NS, 64, 256), velocity.reshape(3, 64, 256), diffusivity[None, :], log_rates, reactants.T, products.T, jnp.transpose(substeps, (0, 2, 1)))
 
 
 def kinetics_kernel(G, order_ref, size_ref, mov_hbm, weight_hbm, s1_hbm, s2_hbm, out_ref, heat_ref, mov, cur, outs, weight_ref, s1_ref, s2_ref, sem, arrive):
@@ -249,7 +254,7 @@
             return 0
         lax.fori_loop(0, ns[0], level, 0)
         for j in range(G):
-            c, z = ids[j] // 2, ids[j] % 2
+            c, z = ids[j] % 64, ids[j] // 64
             res = cur[:, j * 128:(j + 1) * 128]
             outs[z, pl.ds(c, NS, stride=64), :] = res[:NS]
             heat_ref[z, pl.ds(c, 1), :] = jnp.sum(weight * (res - mov[slot, j]), axis=0, keepdims=True)
@@ -437,7 +442,7 @@
 
 
 def local(species, velocity, diffusivity, divergence, log_rates, reactants, products, heat_weights, substeps):
-    moved, first, second, order = advance(species, velocity, diffusivity, log_rates, reactants, products, substeps.reshape(-1))
+    moved, first, second, order = advance(species, velocity, diffusivity, log_rates, reactants, products, substeps)
     reacted, heat = kinetics(16, moved, order, heat_weights, first, second)
     pressure = solve(heat, divergence)
     return reacted.reshape(species.shape), pressure

time: 109 us -> 101 us (0.927)
  local copies, waits for them, and re-layouts: 7.53 us -> 1.47 us
    pallas_call x1, Pallas kernels: 55.1 us -> 28.4 us  [solve(): pl.pallas_call(solve_kernel, out_shape=jax.ShapeDtypeStruct((64, 256), f3...]
    pallas_call x1, Pallas kernels: 21.6 us -> 47.2 us  [kinetics(): pl.pallas_call(functools.partial(kinetics_kernel, G), out_shape=(jax.Shap...]
    unnamed x4 -> x1, local copies, waits for them, and re-layouts: 5.63 us -> 1.47 us
    broadcast_in_dim x1 -> x0, local copies, waits for them, and re-layouts: 1.25 us -> none  [advance(): log_rates[None, :]]
where the time goes in v3:
time: 101 us
  Pallas kernels  99.1 us (98%)
  local copies, waits for them, and re-layouts  1.47 us (1%)
    pallas_call x1, Pallas kernels, kinetics(): pl.pallas_call(functools.partial(kinetics_kernel, G), out_shape=(jax.Shap...  47.2 us
    pallas_call x1, Pallas kernels, solve(): pl.pallas_call(solve_kernel, out_shape=jax.ShapeDtypeStruct((64, 256), f3...  28.4 us
    pallas_call x1, Pallas kernels, advance(): pl.pallas_call(advance_kernel, out_shape=(shape((128, SP, 128), f32), sha...  23.5 us

profile of v3, /device:TPU:1, one launch (start us, length us, event | category | flops | bytes accessed | tf_op | source)
XLA Modules:
  0.0 101.3 jit_solution(6937777396408548797)
XLA Ops:
  0.6 23.5 %advance.1 = (f32[128,56,128]{2,1,0:T(8,128)}, bf16[336,112]{1,0:T(8,128)(2,1)}, bf16[112,672]{1,0:T(8,128)(2,1)}, s32[2,128]{1,0:T(2,128)}) custom-call(f32[53,64,256]{2,1,0:T(8,128)} %bitcast.10, f32[3,64,256]{2,1,0:T(8,128)} %bitcast.12, f32[1,53]{1,0:T(1,128)} %bitcast.17, f32[325]{0:T(512)} %rates_hbm.1, s32[53,325]{1,0:T(8,128)} %bitcast.13, ...), custom_call_target="tpu_custom_call" | custom-call | tf_op jit(solution)/shard_map/advance/pallas_call | solution.py:198
  24.2 47.2 %kinetics.1 = (f32[3392,256]{1,0:T(8,128)}, f32[2,64,128]{2,1,0:T(8,128)}) custom-call(s32[2,128]{1,0:T(2,128)} %get-tuple-element.8.order_ref, f32[8]{0:T(128)} %constant.12.clone.size_ref, f32[128,56,128]{2,1,0:T(8,128)} %get-tuple-element.9.mov_hbm, f32[1,53]{1,0:T(1,128)} %bitcast.18, bf16[336,112]{1,0:T(8,128)(2,1)} %get-tuple-element.10.s1_hbm, ...), custom_call_target="tpu_custom_call" | custom-call | tf_op jit(solution)/shard_map/kinetics/pallas_call | solution.py:275
  71.3 28.4 %screened_solve.1 = f32[64,256]{1,0:T(8,128)} custom-call(f32[2,64,128]{2,1,0:T(8,128)} %get-tuple-element.13.heat_hbm, f32[64,256]{1,0:T(8,128)} %bitcast.15, f32[256,256]{1,0:T(8,128)} %constant.13.clone.tz_hbm, f32[64,64]{1,0:T(8,128)} %constant.14.clone.tx_hbm, f32[128,128]{1,0:T(8,128)} %constant.15.clone.ty_hbm, f32[128,128]{1,0:T(8,128)} %constant.16.clone.shift_hbm, ...), custom_call_target="tpu_custom_call" | custom-call | tf_op jit(solution)/shard_map/screened_solve/pallas_call | solution.py:425
  99.8 1.5 %copy.18 = f32[8,8,256]{2,1,0:T(8,128)} copy(f32[8,8,256]{2,1,0:T(8,128)} %bitcast.11) | data formatting | bytes 131072

commit v4 on v3

--- a/solution.py
+++ b/solution.py
@@ -58,7 +58,7 @@
 
 
 def advance_kernel(species, vel_hbm, diff_hbm, rates_hbm, react_hbm, prod_hbm, counts_hbm, mov_ref, first_ref, second_ref, order_ref,
-                   sp, hx, ext, mv, vel_ref, diff_ref, rates_ref, react_ref, prod_ref, counts_ref, react, prod, halves, sem_in, ss, rs, sem_out):
+                   hx, ext, mv, vel_ref, diff_ref, rates_ref, react_ref, prod_ref, counts_ref, react, prod, halves, sem_in, ss, rs, sem_out):
     rows, cols = lax.axis_size("row"), lax.axis_size("col")
     me_r, me_c = lax.axis_index("row"), lax.axis_index("col")
     above = {"row": lax.rem(me_r + 1, rows), "col": me_c}
@@ -68,10 +68,22 @@
     barrier = pltpu.get_barrier_semaphore()
     for peer in (above, below, right, left):
         pl.semaphore_signal(barrier, inc=1, device_id=peer, device_id_type=MESH)
-    loads = [pltpu.make_async_copy(species.at[:, :, pl.ds(z * 128, 128)], sp.at[z], sem_in.at[z]) for z in range(2)]
-    loads += [pltpu.make_async_copy(vel_hbm, vel_ref, sem_in.at[2]), pltpu.make_async_copy(diff_hbm, diff_ref, sem_in.at[3])]
-    extra = [pltpu.make_async_copy(a, b, sem_in.at[4 + k]) for k, (a, b) in enumerate(((rates_hbm, rates_ref), (react_hbm, react_ref), (prod_hbm, prod_ref), (counts_hbm, counts_ref)))]
-    for c in loads + extra:
+    def column(x, y, z, sem):
+        zs = pl.ds(z * 128, 128)
+        return pltpu.make_async_copy(species.at[:, x * 8 + y, zs], ext.at[x + 1, y + 1, z, pl.ds(0, NS)], sem)
+
+    def arrived(count, sem):
+        whole = mv.at[pl.ds(0, count), pl.ds(0, NS)]
+        pltpu.make_async_copy(whole, whole, sem).wait()
+
+    def edge_columns(x, _):
+        for y in (0, 7):
+            for z in range(2):
+                column(x, y, z, sem_in.at[0]).start()
+        return 0
+    lax.fori_loop(0, 8, edge_columns, 0)
+    extra = [pltpu.make_async_copy(a, b, sem_in.at[9 + k]) for k, (a, b) in enumerate(((vel_hbm, vel_ref), (diff_hbm, diff_ref), (rates_hbm, rates_ref), (react_hbm, react_ref), (prod_hbm, prod_ref), (counts_hbm, counts_ref)))]
+    for c in extra:
         c.start()
     pl.semaphore_wait(barrier, 4)
     x_copies = []
@@ -81,33 +93,20 @@
         x_copies.append(pltpu.make_async_remote_copy(src_ref=species.at[:, pl.ds(0, 8), zs], dst_ref=hx.at[1, z], send_sem=ss.at[4 + z], recv_sem=rs.at[4 + z], device_id=below, device_id_type=MESH))
     for c in x_copies:
         c.start()
-    for c in loads:
-        c.wait()
-
-    def lay(x, y):
-        c = x * 8 + y
-        for z in range(2):
-            ext[x + 1, y + 1, :NS, z * 128:(z + 1) * 128] = sp_rows(z, c)
-
-    def sp_rows(z, c):
-        return sp.at[z].reshape(NS * 64, 128)[pl.ds(c, NS, stride=64), :]
-
-    def lay_edge(x, _):
-        lay(x, 0)
-        lay(x, 7)
-        return 0
-    lax.fori_loop(0, 8, lay_edge, 0)
+    def inner_columns(x, _):
+        for y in range(1, 7):
+            for z in range(2):
+                column(x, y, z, sem_in.at[1 + x]).start()
+        return 0
+    lax.fori_loop(0, 8, inner_columns, 0)
+    arrived(32, sem_in.at[0])
     y_up = pltpu.make_async_remote_copy(src_ref=ext.at[pl.ds(1, 8), 8], dst_ref=ext.at[pl.ds(1, 8), 0], send_sem=ss.at[0], recv_sem=rs.at[0], device_id=right, device_id_type=MESH)
     y_down = pltpu.make_async_remote_copy(src_ref=ext.at[pl.ds(1, 8), 1], dst_ref=ext.at[pl.ds(1, 8), 9], send_sem=ss.at[1], recv_sem=rs.at[1], device_id=left, device_id_type=MESH)
     y_up.start()
     y_down.start()
 
-    def lay_inner(x, _):
-        for y in range(1, 7):
-            lay(x, y)
-        return 0
-    lax.fori_loop(0, 8, lay_inner, 0)
-
+    for c in extra:
+        c.wait()
     own = lax.broadcasted_iota(jnp.int32, (SP, NS), 0) == lax.broadcasted_iota(jnp.int32, (SP, NS), 1)
     fifth = jnp.broadcast_to(0.2 * jnp.sum(jnp.where(own, diff_ref[...], 0.0), axis=1, keepdims=True), (SP, 256))
     lane = lax.broadcasted_iota(jnp.int32, (SP, 256), 1)
@@ -115,8 +114,10 @@
 
     def move(x, y):
         c = x * 8 + y
-        centre = ext[x + 1, y + 1]
-        near = (ext[x, y + 1], ext[x + 2, y + 1], ext[x + 1, y], ext[x + 1, y + 2],
+        def cells(at, to):
+            return jnp.concatenate([ext[at, to, 0], ext[at, to, 1]], axis=1)
+        centre = cells(x + 1, y + 1)
+        near = (cells(x, y + 1), cells(x + 2, y + 1), cells(x + 1, y), cells(x + 1, y + 2),
                 jnp.where(lane == 0, centre, pltpu.roll(centre, 1, 1)), jnp.where(lane == 255, centre, pltpu.roll(centre, 255, 1)))
         speeds = [0.2 * vel_ref[d, pl.ds(c, 1), :] for d in range(3)]
         still = 1.0 - (jnp.abs(speeds[0]) + jnp.abs(speeds[1]) + jnp.abs(speeds[2]))
@@ -128,14 +129,17 @@
         mv[c] = total[:, :128]
         mv[64 + c] = total[:, 128:]
 
+    arrived(12, sem_in.at[1])
+    arrived(12, sem_in.at[2])
+
     def inner(x, _):
+        arrived(12, sem_in.at[2 + x])
+
         def go(y, _):
             move(x, y)
             return 0
         return lax.fori_loop(1, 7, go, 0)
     lax.fori_loop(1, 7, inner, 0)
-    for c in extra:
-        c.wait()
     build_matrices(rates_ref, react_ref, prod_ref, react, prod, halves, first_ref, second_ref)
     build_order(counts_ref, order_ref)
     y_up.wait()
@@ -163,7 +167,7 @@
     def lay_halo(y, _):
         for k, at in ((0, 0), (1, 9)):
             for z in range(2):
-                ext[at, y + 1, :NS, z * 128:(z + 1) * 128] = hx_rows(k, z, y)
+                ext[at, y + 1, z, :NS, :] = hx_rows(k, z, y)
         return 0
 
     def hx_rows(k, z, y):
@@ -200,19 +204,26 @@
         out_shape=(shape((128, SP, 128), f32), shape((RP, 2 * SP), bf16), shape((2 * SP, 2 * RP), bf16), shape((2, 128), jnp.int32)),
         in_specs=[hb] * 7,
         out_specs=(hb, vm, vm, vm),
-        scratch_shapes=[pltpu.VMEM((2, NS, 64, 128), f32), pltpu.VMEM((2, 2, NS, 8, 128), f32), pltpu.VMEM((10, 10, SP, 256), f32), pltpu.VMEM((128, SP, 128), f32),
+        scratch_shapes=[pltpu.VMEM((2, 2, NS, 8, 128), f32), pltpu.VMEM((10, 10, 2, SP, 128), f32), pltpu.VMEM((128, SP, 128), f32),
                         pltpu.VMEM((3, 64, 256), f32), pltpu.VMEM((1, NS), f32), pltpu.VMEM((NR,), f32), pltpu.VMEM((NS, NR), jnp.int32), pltpu.VMEM((NS, NR), jnp.int32),
-                        pltpu.VMEM((8, 2, 8), jnp.int32), pltpu.VMEM((128, 384), f32), pltpu.VMEM((128, 384), f32), pltpu.VMEM((2 * SP, RP + 384), f32), dma((8,)), dma((6,)), dma((6,)), dma((6,))],
+                        pltpu.VMEM((8, 2, 8), jnp.int32), pltpu.VMEM((128, 384), f32), pltpu.VMEM((128, 384), f32), pltpu.VMEM((2 * SP, RP + 384), f32), dma((15,)), dma((6,)), dma((6,)), dma((6,))],
         compiler_params=pltpu.CompilerParams(collective_id=0, has_side_effects=True, vmem_limit_bytes=60 << 20),
         name="advance",
     )(species.reshape(NS, 64, 256), velocity.reshape(3, 64, 256), diffusivity[None, :], log_rates, reactants.T, products.T, jnp.transpose(substeps, (0, 2, 1)))
 
 
-def kinetics_kernel(G, order_ref, size_ref, mov_hbm, weight_hbm, s1_hbm, s2_hbm, out_ref, heat_ref, mov, cur, outs, weight_ref, s1_ref, s2_ref, sem, arrive):
+def kinetics_kernel(G, order_ref, size_ref, mov_hbm, weight_hbm, s1_hbm, s2_hbm, out_ref, heat_ref, mov, cur, stage, depart, weight_ref, s1_ref, s2_ref, sem, arrive):
     turns = 128 // G
 
     def fetch(t, slot):
         return [pltpu.make_async_copy(mov_hbm.at[order_ref[0, t * G + j]], mov.at[slot, j], arrive.at[slot]) for j in range(G)]
+    def leave(t, slot):
+        made = []
+        for j in range(G):
+            i = order_ref[0, t * G + j]
+            made.append(pltpu.make_async_copy(stage.at[slot, j, pl.ds(0, NS)], out_ref.at[:, i % 64, pl.ds(pl.multiple_of(i // 64 * 128, 128), 128)], depart.at[slot]))
+        return made
+
     for c in fetch(0, 0):
         c.start()
     constants = [pltpu.make_async_copy(a, b, sem.at[k]) for k, (a, b) in enumerate(((weight_hbm, weight_ref), (s1_hbm, s1_ref), (s2_hbm, s2_ref)))]
@@ -253,18 +264,22 @@
             cur[...] = jnp.where(nb > k, fresh, conc)
             return 0
         lax.fori_loop(0, ns[0], level, 0)
+        @pl.when(t >= 2)
+        def _():
+            for c in leave(t, slot):
+                c.wait()
         for j in range(G):
             c, z = ids[j] % 64, ids[j] // 64
             res = cur[:, j * 128:(j + 1) * 128]
-            outs[z, pl.ds(c, NS, stride=64), :] = res[:NS]
+            stage[slot, j] = res
             heat_ref[z, pl.ds(c, 1), :] = jnp.sum(weight * (res - mov[slot, j]), axis=0, keepdims=True)
+        for c in leave(t, slot):
+            c.start()
         return 0
     lax.fori_loop(0, turns, turn, 0)
-    stores = [pltpu.make_async_copy(outs.at[z], out_ref.at[:, pl.ds(z * 128, 128)], sem.at[z]) for z in range(2)]
-    for c in stores:
-        c.start()
-    for c in stores:
-        c.wait()
+    for slot in range(2):
+        for c in leave(slot, slot):
+            c.wait()
 
 
 def kinetics(G, moved, order, heat_weights, first, second):
@@ -274,11 +289,11 @@
     sizes = np.array([0.0] + [time_step / n for n in range(1, 8)], np.float32)
     return pl.pallas_call(
         functools.partial(kinetics_kernel, G),
-        out_shape=(jax.ShapeDtypeStruct((NS * 64, 256), f32), jax.ShapeDtypeStruct((2, 64, 128), f32)),
+        out_shape=(jax.ShapeDtypeStruct((NS, 64, 256), f32), jax.ShapeDtypeStruct((2, 64, 128), f32)),
         in_specs=[sm, sm, hb, hb, hb, hb],
         out_specs=(hb, vm),
         scratch_shapes=[
-            pltpu.VMEM((2, G, SP, 128), f32), pltpu.VMEM((SP, G * 128), f32), pltpu.VMEM((2, NS * 64, 128), f32), pltpu.VMEM((1, NS), f32),
+            pltpu.VMEM((2, G, SP, 128), f32), pltpu.VMEM((SP, G * 128), f32), pltpu.VMEM((2, G, SP, 128), f32), pltpu.SemaphoreType.DMA((2,)), pltpu.VMEM((1, NS), f32),
             pltpu.VMEM((RP, 2 * SP), bf16), pltpu.VMEM((2 * SP, 2 * RP), bf16), pltpu.SemaphoreType.DMA((3,)), pltpu.SemaphoreType.DMA((2,))],
         compiler_params=pltpu.CompilerParams(vmem_limit_bytes=60 << 20),
         name="kinetics",

time: 101 us -> 98.4 us (0.974)
  Pallas kernels: 99.1 us -> 96 us
    pallas_call x1, Pallas kernels: 47.2 us -> 17.8 us  [kinetics(): pl.pallas_call(functools.partial(kinetics_kernel, G), out_shape=(jax.Shap...]
    pallas_call x1, Pallas kernels: 28.4 us -> 54.6 us  [solve(): pl.pallas_call(solve_kernel, out_shape=jax.ShapeDtypeStruct((64, 256), f3...]
where the time goes in v4:
time: 98.4 us; the launch traced here: 98.1 us
  Pallas kernels  96 us (98%)
  local copies, waits for them, and re-layouts  1.47 us (1%)
    pallas_call x1, Pallas kernels, solve(): pl.pallas_call(solve_kernel, out_shape=jax.ShapeDtypeStruct((64, 256), f3...  54.6 us
    pallas_call x1, Pallas kernels, advance(): pl.pallas_call(advance_kernel, out_shape=(shape((128, SP, 128), f32), sha...  23.6 us
    pallas_call x1, Pallas kernels, kinetics(): pl.pallas_call(functools.partial(kinetics_kernel, G), out_shape=(jax.Shap...  17.8 us

profile of v4, /device:TPU:1, one launch (start us, length us, event | category | flops | bytes accessed | tf_op | source)
XLA Modules:
  0.0 98.1 jit_solution(10189692322954437140)
XLA Ops:
  0.6 23.6 %advance.1 = (f32[128,56,128]{2,1,0:T(8,128)}, bf16[336,112]{1,0:T(8,128)(2,1)}, bf16[112,672]{1,0:T(8,128)(2,1)}, s32[2,128]{1,0:T(2,128)}) custom-call(f32[53,64,256]{2,1,0:T(8,128)} %bitcast.10, f32[3,64,256]{2,1,0:T(8,128)} %bitcast.12, f32[1,53]{1,0:T(1,128)} %bitcast.17, f32[325]{0:T(512)} %rates_hbm.1, s32[53,325]{1,0:T(8,128)} %bitcast.13, ...), custom_call_target="tpu_custom_call" | custom-call | tf_op jit(solution)/shard_map/advance/pallas_call | solution.py:202
  24.2 17.8 %kinetics.1 = (f32[53,64,256]{2,1,0:T(8,128)}, f32[2,64,128]{2,1,0:T(8,128)}) custom-call(s32[2,128]{1,0:T(2,128)} %get-tuple-element.8.order_ref, f32[8]{0:T(128)} %constant.12.clone.size_ref, f32[128,56,128]{2,1,0:T(8,128)} %get-tuple-element.9.mov_hbm, f32[1,53]{1,0:T(1,128)} %bitcast.18, bf16[336,112]{1,0:T(8,128)(2,1)} %get-tuple-element.10.s1_hbm, ...), custom_call_target="tpu_custom_call" | custom-call | tf_op jit(solution)/shard_map/kinetics/pallas_call | solution.py:290
  42.0 54.6 %screened_solve.1 = f32[64,256]{1,0:T(8,128)} custom-call(f32[2,64,128]{2,1,0:T(8,128)} %get-tuple-element.13.heat_hbm, f32[64,256]{1,0:T(8,128)} %bitcast.15, f32[256,256]{1,0:T(8,128)} %constant.13.clone.tz_hbm, f32[64,64]{1,0:T(8,128)} %constant.14.clone.tx_hbm, f32[128,128]{1,0:T(8,128)} %constant.15.clone.ty_hbm, f32[128,128]{1,0:T(8,128)} %constant.16.clone.shift_hbm, ...), custom_call_target="tpu_custom_call" | custom-call | tf_op jit(solution)/shard_map/screened_solve/pallas_call | solution.py:440
  96.6 1.5 %copy.18 = f32[8,8,256]{2,1,0:T(8,128)} copy(f32[8,8,256]{2,1,0:T(8,128)} %bitcast.11) | data formatting | bytes 131072

commit v5 on v4

--- a/solution.py
+++ b/solution.py
@@ -16,6 +16,8 @@
 time_step = 0.2
 screen = 0.004
 highest = lax.Precision.HIGHEST
+FAR_ROW = (6, 2, 5, 3, 4, 7, 1)
+FAR_COL = (12, 10, 14, 8, 11, 13, 9, 15, 4, 6, 2, 5, 3, 7, 1)
 
 def split3(x):
     hi = x.astype(bf16).astype(f32)
@@ -112,22 +114,26 @@
     lane = lax.broadcasted_iota(jnp.int32, (SP, 256), 1)
     row = lax.broadcasted_iota(jnp.int32, (SP, 256), 0)
 
-    def move(x, y):
+    def move(x, y, halves=slice(0, 256)):
         c = x * 8 + y
+        low, high = halves.start // 128, halves.stop // 128
+
         def cells(at, to):
-            return jnp.concatenate([ext[at, to, 0], ext[at, to, 1]], axis=1)
-        centre = cells(x + 1, y + 1)
+            return jnp.concatenate([ext[at, to, z] for z in range(low, high)], axis=1)
+        whole = jnp.concatenate([ext[x + 1, y + 1, 0], ext[x + 1, y + 1, 1]], axis=1)
+        centre = whole[:, halves]
+        diffused, lanes, rows_here = fifth[:, halves], lane[:, halves], row[:, halves]
         near = (cells(x, y + 1), cells(x + 2, y + 1), cells(x + 1, y), cells(x + 1, y + 2),
-                jnp.where(lane == 0, centre, pltpu.roll(centre, 1, 1)), jnp.where(lane == 255, centre, pltpu.roll(centre, 255, 1)))
-        speeds = [0.2 * vel_ref[d, pl.ds(c, 1), :] for d in range(3)]
+                jnp.where(lanes == 0, centre, pltpu.roll(whole, 1, 1)[:, halves]), jnp.where(lanes == 255, centre, pltpu.roll(whole, 255, 1)[:, halves]))
+        speeds = [0.2 * vel_ref[d, pl.ds(c, 1), :][:, halves] for d in range(3)]
         still = 1.0 - (jnp.abs(speeds[0]) + jnp.abs(speeds[1]) + jnp.abs(speeds[2]))
-        total = centre * (still - 6.0 * fifth)
+        total = centre * (still - 6.0 * diffused)
         for d in range(3):
-            total = total + near[2 * d] * (fifth + jnp.maximum(speeds[d], 0.0))
-            total = total + near[2 * d + 1] * (fifth - jnp.minimum(speeds[d], 0.0))
-        total = jnp.where(row < NS, total, 2.0)
-        mv[c] = total[:, :128]
-        mv[64 + c] = total[:, 128:]
+            total = total + near[2 * d] * (diffused + jnp.maximum(speeds[d], 0.0))
+            total = total + near[2 * d + 1] * (diffused - jnp.minimum(speeds[d], 0.0))
+        total = jnp.where(rows_here < NS, total, 2.0)
+        for z in range(low, high):
+            mv[64 * z + c] = total[:, (z - low) * 128:(z - low + 1) * 128]
 
     arrived(12, sem_in.at[1])
     arrived(12, sem_in.at[2])
@@ -161,35 +167,33 @@
     middle = [pltpu.make_async_copy(mv.at[pl.ds(64 * z + 8, 48)], mov_ref.at[pl.ds(64 * z + 8, 48)], sem_out.at[z]) for z in range(2)]
     for c in middle:
         c.start()
-    for c in x_copies:
-        c.wait()
-
-    def lay_halo(y, _):
-        for k, at in ((0, 0), (1, 9)):
-            for z in range(2):
-                ext[at, y + 1, z, :NS, :] = hx_rows(k, z, y)
-        return 0
-
-    def hx_rows(k, z, y):
-        return hx.at[k, z].reshape(NS * 8, 128)[pl.ds(y, NS, stride=8), :]
-    lax.fori_loop(0, 8, lay_halo, 0)
-
-    @pl.when(me_r == 0)
-    def _():
-        ext[0, pl.ds(1, 8)] = ext[1, pl.ds(1, 8)]
-
-    @pl.when(me_r == rows - 1)
-    def _():
-        ext[9, pl.ds(1, 8)] = ext[8, pl.ds(1, 8)]
-
-    def ends(y, _):
-        move(0, y)
-        move(7, y)
-        return 0
-    lax.fori_loop(0, 8, ends, 0)
-    outer = [pltpu.make_async_copy(mv.at[pl.ds(at, 8)], mov_ref.at[pl.ds(at, 8)], sem_out.at[2 + k]) for k, at in enumerate((0, 56, 64, 120))]
-    for c in outer:
-        c.start()
+    outer = []
+    for z in range(2):
+        for c in x_copies[2 * z:2 * z + 2]:
+            c.wait()
+
+        def lay_halo(y, _):
+            for k, at in ((0, 0), (1, 9)):
+                ext[at, y + 1, z, :NS, :] = hx.at[k, z].reshape(NS * 8, 128)[pl.ds(y, NS, stride=8), :]
+            return 0
+        lax.fori_loop(0, 8, lay_halo, 0)
+
+        @pl.when(me_r == 0)
+        def _():
+            ext[0, pl.ds(1, 8), z] = ext[1, pl.ds(1, 8), z]
+
+        @pl.when(me_r == rows - 1)
+        def _():
+            ext[9, pl.ds(1, 8), z] = ext[8, pl.ds(1, 8), z]
+
+        def ends(y, _):
+            move(0, y, slice(z * 128, (z + 1) * 128))
+            move(7, y, slice(z * 128, (z + 1) * 128))
+            return 0
+        lax.fori_loop(0, 8, ends, 0)
+        for k, at in ((0, 64 * z), (1, 64 * z + 56)):
+            outer.append(pltpu.make_async_copy(mv.at[pl.ds(at, 8)], mov_ref.at[pl.ds(at, 8)], sem_out.at[2 + 2 * z + k]))
+            outer[-1].start()
     for c in middle + outer:
         c.wait()
 
@@ -224,6 +228,10 @@
             made.append(pltpu.make_async_copy(stage.at[slot, j, pl.ds(0, NS)], out_ref.at[:, i % 64, pl.ds(pl.multiple_of(i // 64 * 128, 128), 128)], depart.at[slot]))
         return made
 
+    def left(slot):
+        whole = stage.at[slot, :, pl.ds(0, NS)]
+        pltpu.make_async_copy(whole, whole, depart.at[slot]).wait()
+
     for c in fetch(0, 0):
         c.start()
     constants = [pltpu.make_async_copy(a, b, sem.at[k]) for k, (a, b) in enumerate(((weight_hbm, weight_ref), (s1_hbm, s1_ref), (s2_hbm, s2_ref)))]
@@ -244,8 +252,7 @@
                 c.start()
         ids = [order_ref[0, t * G + j] for j in range(G)]
         ns = [order_ref[1, t * G + j] for j in range(G)]
-        for c in fetch(t, slot):
-            c.wait()
+        pltpu.make_async_copy(mov.at[slot], mov.at[slot], arrive.at[slot]).wait()
         for j in range(G):
             cur[:, j * 128:(j + 1) * 128] = mov[slot, j]
         h = jnp.concatenate([jnp.full((SP, 128), size_ref[n], f32) for n in ns], axis=1)
@@ -266,20 +273,18 @@
         lax.fori_loop(0, ns[0], level, 0)
         @pl.when(t >= 2)
         def _():
-            for c in leave(t, slot):
-                c.wait()
+            left(slot)
         for j in range(G):
-            c, z = ids[j] % 64, ids[j] // 64
-            res = cur[:, j * 128:(j + 1) * 128]
-            stage[slot, j] = res
-            heat_ref[z, pl.ds(c, 1), :] = jnp.sum(weight * (res - mov[slot, j]), axis=0, keepdims=True)
+            stage[slot, j] = cur[:, j * 128:(j + 1) * 128]
         for c in leave(t, slot):
             c.start()
+        for j in range(G):
+            term = weight * (cur[:, j * 128:(j + 1) * 128] - mov[slot, j])
+            heat_ref[ids[j] // 64, pl.ds(ids[j] % 64, 1), :] = jnp.sum(term, axis=0, keepdims=True)
         return 0
     lax.fori_loop(0, turns, turn, 0)
-    for slot in range(2):
-        for c in leave(slot, slot):
-            c.wait()
+    left(0)
+    left(1)
 
 
 def kinetics(G, moved, order, heat_weights, first, second):
@@ -369,7 +374,7 @@
                     tile = jnp.where(part == p, pltpu.roll(v[p], s, 1) if s else v[p], tile)
                 send1[kh * 4 + q, :, h * 128:(h + 1) * 128] = tile
     pl.semaphore_wait(barrier, rows - 1 + cols - 1)
-    sent = [row_copy(send1, recv1, ss1, rs1, d) for d in range(1, rows)]
+    sent = [row_copy(send1, recv1, ss1, rs1, d) for d in FAR_ROW]
     for c in sent:
         c.start()
     recv1[me_r] = send1[me_r]
@@ -382,7 +387,7 @@
     yv[...] = exact_dot(jnp.transpose(block), jnp.concatenate([tx, tx], axis=0), ((1,), (1,)))
     for c in range(cols):
         send2[c] = jnp.where(lane < 64, yv[pl.ds(2 * c, 8, stride=32), :], yv[pl.ds(2 * c + 1, 8, stride=32), :])
-    sent = [col_copy(send2, recv2, ss2, rs2, d) for d in range(1, cols)]
+    sent = [col_copy(send2, recv2, ss2, rs2, d) for d in FAR_COL]
     for c in sent:
         c.start()
     recv2[me_c] = send2[me_c]
@@ -395,7 +400,7 @@
     shift = shift_ref[pl.ds(me_r * cols + me_c, 1), :]
     spectrum = spectrum / (ly_ref[...] + shift)
     send2[...] = exact_dot(ty, spectrum, ((0,), (0,))).reshape(cols, 8, 128)
-    sent = [col_copy(send2, recv3, ss3, rs3, d) for d in range(1, cols)]
+    sent = [col_copy(send2, recv3, ss3, rs3, d) for d in FAR_COL]
     for c in sent:
         c.start()
     recv3[me_c] = send2[me_c]
@@ -409,7 +414,7 @@
         yb[pl.ds(2 * c + 1, 8, stride=32), :] = jnp.where(lane < 64, 0.0, tile)
     txt = jnp.transpose(tx)
     send4[...] = exact_dot(jnp.concatenate([txt, txt], axis=1), yb[...], ((1,), (1,))).reshape(8, 8, 256)
-    sent = [row_copy(send4, recv4, ss4, rs4, d) for d in range(1, rows)]
+    sent = [row_copy(send4, recv4, ss4, rs4, d) for d in FAR_ROW]
     for c in sent:
         c.start()
     recv4[me_r] = send4[me_r]

time: 98.4 us -> 97.2 us (0.988)
    pallas_call x1, Pallas kernels: 54.6 us -> 40.9 us  [solve(): pl.pallas_call(solve_kernel, out_shape=jax.ShapeDtypeStruct((64, 256), f3...]
    pallas_call x1, Pallas kernels: 17.8 us -> 31.1 us  [kinetics(): pl.pallas_call(functools.partial(kinetics_kernel, G), out_shape=(jax.Shap...]
where the time goes in v5:
time: 97.2 us
  Pallas kernels  95.1 us (98%)
  local copies, waits for them, and re-layouts  1.47 us (2%)
    pallas_call x1, Pallas kernels, solve(): pl.pallas_call(solve_kernel, out_shape=jax.ShapeDtypeStruct((64, 256), f3...  40.9 us
    pallas_call x1, Pallas kernels, kinetics(): pl.pallas_call(functools.partial(kinetics_kernel, G), out_shape=(jax.Shap...  31.1 us
    pallas_call x1, Pallas kernels, advance(): pl.pallas_call(advance_kernel, out_shape=(shape((128, SP, 128), f32), sha...  23.1 us

profile of v5, /device:TPU:1, one launch (start us, length us, event | category | flops | bytes accessed | tf_op | source)
XLA Modules:
  0.0 97.2 jit_solution(15968550814427199367)
XLA Ops:
  0.6 23.1 %advance.1 = (f32[128,56,128]{2,1,0:T(8,128)}, bf16[336,112]{1,0:T(8,128)(2,1)}, bf16[112,672]{1,0:T(8,128)(2,1)}, s32[2,128]{1,0:T(2,128)}) custom-call(f32[53,64,256]{2,1,0:T(8,128)} %bitcast.10, f32[3,64,256]{2,1,0:T(8,128)} %bitcast.12, f32[1,53]{1,0:T(1,128)} %bitcast.17, f32[325]{0:T(512)} %rates_hbm.1, s32[53,325]{1,0:T(8,128)} %bitcast.13, ...), custom_call_target="tpu_custom_call" | custom-call | tf_op jit(solution)/shard_map/advance/pallas_call | solution.py:206
  23.7 31.1 %kinetics.1 = (f32[53,64,256]{2,1,0:T(8,128)}, f32[2,64,128]{2,1,0:T(8,128)}) custom-call(s32[2,128]{1,0:T(2,128)} %get-tuple-element.8.order_ref, f32[8]{0:T(128)} %constant.12.clone.size_ref, f32[128,56,128]{2,1,0:T(8,128)} %get-tuple-element.9.mov_hbm, f32[1,53]{1,0:T(1,128)} %bitcast.18, bf16[336,112]{1,0:T(8,128)(2,1)} %get-tuple-element.10.s1_hbm, ...), custom_call_target="tpu_custom_call" | custom-call | tf_op jit(solution)/shard_map/kinetics/pallas_call | solution.py:295
  54.8 40.9 %screened_solve.1 = f32[64,256]{1,0:T(8,128)} custom-call(f32[2,64,128]{2,1,0:T(8,128)} %get-tuple-element.13.heat_hbm, f32[64,256]{1,0:T(8,128)} %bitcast.15, f32[256,256]{1,0:T(8,128)} %constant.13.clone.tz_hbm, f32[64,64]{1,0:T(8,128)} %constant.14.clone.tx_hbm, f32[128,128]{1,0:T(8,128)} %constant.15.clone.ty_hbm, f32[128,128]{1,0:T(8,128)} %constant.16.clone.shift_hbm, ...), custom_call_target="tpu_custom_call" | custom-call | tf_op jit(solution)/shard_map/screened_solve/pallas_call | solution.py:445
  95.7 1.5 %copy.18 = f32[8,8,256]{2,1,0:T(8,128)} copy(f32[8,8,256]{2,1,0:T(8,128)} %bitcast.11) | data formatting | bytes 131072
